TPU v7x, 32 devices: a whole 2x2x4 slice. The times are simulated.
32 devices in a mesh: seq: 4 (over y, x), fsdp: 8 (over z, core).
Axes of the slice: x: 2, y: 2, z: 4, core: 2. Of those that a mesh axis runs over, the one named last changes fastest.
Arguments:
- tokens: bfloat16 [8, 1024, 1280], P('fsdp', 'seq'), may hold values from -6 to 6
- picture_ids: int32 [8, 1024], P('fsdp', 'seq'), may hold values from -1 to 10, as said below
- patch_rows: int32 [8, 1024], P('fsdp', 'seq'), may hold values from 0 to 31, as said below
- patch_cols: int32 [8, 1024], P('fsdp', 'seq'), may hold values from 0 to 31, as said below
- norm1_gain: bfloat16 [1280], P('fsdp'), may hold values from 0.099609375 to 1.8984375
- norm1_bias: bfloat16 [1280], P('fsdp'), may hold values from -3 to 3
- qkv_weight: bfloat16 [1280, 3840], P('fsdp'), may hold values from -0.15625 to 0.15625
- qkv_bias: bfloat16 [3840], P('fsdp'), may hold values from -3 to 3
- proj_weight: bfloat16 [1280, 1280], P('fsdp'), may hold values from -2 to 2
- proj_bias: bfloat16 [1280], P('fsdp'), may hold values from -3 to 3
- norm2_gain: bfloat16 [1280], P('fsdp'), may hold values from 0.099609375 to 1.8984375
- norm2_bias: bfloat16 [1280], P('fsdp'), may hold values from -3 to 3
- fc1_weight: bfloat16 [1280, 5120], P('fsdp'), may hold values from -0.15625 to 0.15625
- fc1_bias: bfloat16 [5120], P('fsdp'), may hold values from -3 to 3
- fc2_weight: bfloat16 [5120, 1280], P('fsdp'), may hold values from -0.078125 to 0.078125
- fc2_bias: bfloat16 [1280], P('fsdp'), may hold values from -3 to 3
- cotangent: bfloat16 [8, 1024, 1280], P('fsdp', 'seq'), may hold values from -6 to 6
Outputs:
- block_out: bfloat16 [8, 1024, 1280], P('fsdp', 'seq')
- tokens_grad: float32 [8, 1024, 1280], P('fsdp', 'seq')
- norm1_gain_grad: float32 [1280], P('fsdp')
- norm1_bias_grad: float32 [1280], P('fsdp')
- qkv_weight_grad: float32 [1280, 3840], P('fsdp')
- qkv_bias_grad: float32 [3840], P('fsdp')
- proj_weight_grad: float32 [1280, 1280], P('fsdp')
- proj_bias_grad: float32 [1280], P('fsdp')
- norm2_gain_grad: float32 [1280], P('fsdp')
- norm2_bias_grad: float32 [1280], P('fsdp')
- fc1_weight_grad: float32 [1280, 5120], P('fsdp')
- fc1_bias_grad: float32 [5120], P('fsdp')
- fc2_weight_grad: float32 [5120, 1280], P('fsdp')
- fc2_bias_grad: float32 [1280], P('fsdp')
Inputs may be any that keep to these rules, and one draw needn't show every extreme that they name: `picture_ids`: each sequence holds whole pictures in turn from its first token: picture number p (0, 1, 2, ...) of h x w patches, h and w from 10 to 32, takes h * w consecutive tokens with id p; only the last picture of a sequence may have fewer than h rows of patches; the tokens after it, fewer than 32, are padding with id -1. The first sequence holds only pictures of 10 x 10 patches. `patch_rows`: the row of a token's patch within its picture, the picture's tokens going row after row; 0 on padding. The last sequence begins with a picture of 32 x 32 patches. `patch_cols`: the column of a token's patch within its picture; 0 on padding.
All inputs are finite; a program needn't handle non-finite values.
Results may differ from a plain program's by a relative error of at most 0.018.
Values may be sent and summed in bfloat16 or wider, within the bound.
A program may use at most 256 MiB of HBM per device.

v0:
```python
import functools

import jax
import jax.numpy as jnp
import numpy as np
from jax import lax
from jax.experimental import pallas as pl
from jax.experimental.pallas import tpu as pltpu
from jax.sharding import PartitionSpec as P

HD = 80
NORM_EPSILON = 1e-06
MASKED = -1e30
BF = jnp.bfloat16
F32 = jnp.float32


def standardize(values_in):
    centre = jnp.mean(values_in, axis=-1, keepdims=True)
    shifted = values_in - centre
    factor = lax.rsqrt(jnp.mean(shifted * shifted, axis=-1, keepdims=True) + NORM_EPSILON)
    return (shifted * factor, factor)


def norm_back(grad_out, normed, factor, gain):
    scaled = grad_out * gain
    return factor * (
        scaled
        - jnp.mean(scaled, axis=-1, keepdims=True)
        - normed * jnp.mean(scaled * normed, axis=-1, keepdims=True)
    )


def rotary_tables(patch_row, patch_col, head_size):
    quarter = head_size // 4
    inverse = jnp.power(10000.0, -jnp.arange(quarter, dtype=F32) / quarter)
    half_angles = jnp.concatenate(
        [
            patch_row.astype(F32)[..., None] * inverse,
            patch_col.astype(F32)[..., None] * inverse,
        ],
        axis=-1,
    )
    angles = jnp.concatenate([half_angles, half_angles], axis=-1)
    return (jnp.cos(angles)[..., None, :], jnp.sin(angles)[..., None, :])


def rotate(values_in, cosine, sine):
    half_size = values_in.shape[-1] // 2
    turned = jnp.concatenate([-values_in[..., half_size:], values_in[..., :half_size]], axis=-1)
    return values_in * cosine + turned * sine


def unrotate(grad_in, cosine, sine):
    half_size = grad_in.shape[-1] // 2
    moved = grad_in * sine
    return grad_in * cosine + jnp.concatenate(
        [moved[..., half_size:], -moved[..., :half_size]], axis=-1
    )


def masked_scores(queries, keys, picture, factor):
    places = jnp.arange(picture.shape[0], dtype=jnp.int32)
    scores = jnp.einsum("qhd,khd->hqk", queries, keys, preferred_element_type=F32) * factor
    allowed = (picture[:, None] == picture[None, :]) & (
        (picture[None, :] >= 0) | (places[:, None] == places[None, :])
    )
    return jnp.where(allowed[None, :, :], scores, MASKED)


def attend(queries, keys, values, picture):
    scores = masked_scores(queries, keys, picture, HD**-0.5)
    row_max = jnp.max(scores, axis=-1, keepdims=True)
    powers = jnp.exp(scores - row_max)
    totals = jnp.sum(powers, axis=-1, keepdims=True)
    weights = (powers / totals).astype(BF)
    mixed = jnp.einsum("hqk,khd->qhd", weights, values, preferred_element_type=F32)
    return mixed.astype(BF), row_max + jnp.log(totals)


def attend_back(queries, keys, values, picture, grad_mixed, log_total):
    factor = HD**-0.5
    scores = masked_scores(queries, keys, picture, factor)
    probs = jnp.exp(scores - log_total)
    weights = probs.astype(BF)
    grad_values = jnp.einsum("hqk,qhd->khd", weights, grad_mixed, preferred_element_type=F32)
    grad_weights = jnp.einsum("qhd,khd->hqk", grad_mixed, values, preferred_element_type=F32)
    centre = jnp.sum(probs * grad_weights, axis=-1, keepdims=True)
    grad_scores = (probs * (grad_weights - centre)).astype(BF)
    grad_queries = jnp.einsum("hqk,khd->qhd", grad_scores, keys, preferred_element_type=F32) * factor
    grad_keys = jnp.einsum("hqk,qhd->khd", grad_scores, queries, preferred_element_type=F32) * factor
    return grad_queries.astype(BF), grad_keys.astype(BF), grad_values.astype(BF)


def dot(left, right):
    return jnp.dot(left, right, preferred_element_type=F32)


def rows_term(left, right):
    return lax.dot_general(left, right, (((0,), (0,)), ((), ())), preferred_element_type=F32)


def contract_back(grad_out, weight):
    return lax.dot_general(grad_out, weight, (((1,), (1,)), ((), ())), preferred_element_type=F32)


def gather(value, axis_name, axis=0):
    return lax.all_gather(value, axis_name, axis=axis, tiled=True)


def scatter_sum(value, axis_name, axis=0):
    return lax.psum_scatter(value, axis_name, scatter_dimension=axis, tiled=True)

MESH = pl.DeviceIdType.MESH


def mm(left, right):
    return jnp.dot(left, right, preferred_element_type=F32)


def mm_nt(left, right):
    return lax.dot_general(left, right, (((1,), (1,)), ((), ())), preferred_element_type=F32)


def mm_tn(left, right):
    return lax.dot_general(left, right, (((0,), (0,)), ((), ())), preferred_element_type=F32)


def lane_pad(value, lanes):
    gap = lanes - value.shape[1]
    if gap == 0:
        return value
    return jnp.concatenate([value, jnp.zeros((value.shape[0], gap), value.dtype)], axis=1)


def moments(value):
    centre = jnp.mean(value, axis=-1, keepdims=True)
    shifted = value - centre
    factor = lax.rsqrt(jnp.mean(shifted * shifted, axis=-1, keepdims=True) + NORM_EPSILON)
    return shifted * factor, factor


def block_kernel(
    dims,
    tok_in,
    cot_in,
    plc_in,
    small_in,
    wave_in,
    wq_in,
    wp_in,
    w1_in,
    w2_in,
    out_ref,
    tgrad_ref,
    rq_ref,
    rp_ref,
    r1_ref,
    r2_ref,
    sums_ref,
    tokb,
    ain,
    cotb,
    plb,
    plt,
    smb,
    vec,
    bqkv,
    cosb,
    sinb,
    wqc,
    wq,
    wp,
    w1,
    w2,
    qkv,
    lse,
    mixc,
    mix,
    mid,
    mlp,
    act,
    dge,
    snd,
    rsr,
    gmd,
    gp,
    dq4,
    dp4,
    d14,
    d24,
    zq3,
    zp3,
    z13,
    z23,
    dkv,
    smg,
    sg8,
    sems,
    local_sems,
):
    n, T, L, D, F, R, hl, P1, CQ, HP = dims
    J = F // 2
    hw = hl * HD
    W = 128
    QW = hl * W
    scale = HD**-0.5
    tile = 256 if D % 256 == 0 else 128
    me = lax.axis_index("seq")
    f = lax.axis_index("fsdp")
    k = f % 2
    j = f // 2
    partner = f + 1 - 2 * k
    seq_to = [(me + o) % n for o in range(n)]
    seq_from = [(me + n - o) % n for o in range(n)]
    z_to = [2 * ((j + d) % J) + k for d in range(J)]
    z_from = [2 * ((j + J - d) % J) + k for d in range(J)]
    used = {"remote": 0, "local": 0}
    leftover = []

    def take(count=1):
        used["remote"] += count
        return used["remote"] - count

    def send(src, dst, where, recv, late=True):
        copy = pltpu.make_async_remote_copy(
            src_ref=src,
            dst_ref=dst,
            send_sem=sems.at[take()],
            recv_sem=sems.at[recv],
            device_id=where,
            device_id_type=MESH,
        )
        copy.start()
        if late:
            leftover.append(copy)
        return copy

    def load(src, dst):
        used["local"] += 1
        copy = pltpu.make_async_copy(src, dst, local_sems.at[used["local"] - 1])
        copy.start()
        return copy

    def band(ref, index, size):
        return ref.at[pl.ds(pl.multiple_of(index * size, size), size)]

    def rows_of(index, size):
        return pl.ds(pl.multiple_of(index * size, size), size)

    def strips(total, step, body):
        def run(s, carry):
            body(rows_of(s, step))
            return carry

        lax.fori_loop(0, total // step, run, 0)

    strip = 32

    raw_q = [load(wq_in.at[:, t * D : (t + 1) * D], d24.at[t]) for t in range(3)]
    raw_1 = [load(w1_in.at[:, c * P1 : (c + 1) * P1], d14.at[c]) for c in range(n)]

    barrier = pltpu.get_barrier_semaphore()
    for o in range(1, n):
        pl.semaphore_signal(barrier, inc=1, device_id={"seq": seq_to[o]}, device_id_type=MESH)
    for o in range(1, F):
        pl.semaphore_signal(barrier, inc=1, device_id={"fsdp": (f + o) % F}, device_id_type=MESH)
    pl.semaphore_wait(barrier, n - 1 + F - 1)

    tok_copies = []
    for o in range(1, n):
        where = {"seq": seq_to[o]}
        c1 = send(plc_in, plb.at[me], where, take())
        c2 = send(tok_in, tokb.at[me], where, take())
        tok_copies.append((c1, c2))
    own_tok = load(tok_in, tokb.at[me])
    own_plc = load(plc_in, plb.at[me])
    own_small = load(small_in, smb.at[f])

    class Weight:
        def __init__(self, src, buf, rows):
            self.buf, self.rows = buf, rows
            self.own = None
            if src is None:
                src = band(buf, f, rows)
            else:
                self.own = load(src, band(buf, f, rows))
            self.near = send(src, band(buf, f, rows), {"fsdp": partner}, take(), late=False)
            self.far = [
                send(src, band(buf, f, rows), {"fsdp": z_to[d]}, take(), late=False)
                for d in range(1, J)
            ]
            self.relayed = []

        def relay(self):
            for d in range(1, J):
                self.far[d - 1].wait_recv()
                part = band(self.buf, z_from[d], self.rows)
                self.relayed.append(send(part, part, {"fsdp": partner}, take(), late=False))

        def finish(self):
            if self.own is not None:
                self.own.wait()
            self.near.wait_recv()
            for copy in self.relayed:
                copy.wait_recv()

        def drain(self):
            for copy in [self.near] + self.far + self.relayed:
                copy.wait_send()

    def cut_columns(target, lines):
        for m in range(n):

            @pl.when(me == m)
            def _():
                target[rows_of(f, R), :] = lane_pad(
                    jnp.concatenate(lines(m), axis=1), target.shape[1]
                )

    small_copies = [
        send(small_in, smb.at[f], {"fsdp": (f + o) % F}, take()) for o in range(1, F)
    ]
    for copy in raw_q:
        copy.wait()
    cut_columns(wqc, lambda m: [d24[t, :, m * hw : (m + 1) * hw] for t in range(3)])
    weight_q = Weight(None, wqc, R)
    weight_p = Weight(wp_in, wp, R)
    for copy in raw_1:
        copy.wait()
    cut_columns(
        w1,
        lambda m: [
            d14[b * n * R // P1, :, b * n * R % P1 + m * R : b * n * R % P1 + (m + 1) * R]
            for b in range(F)
        ],
    )
    weight_1 = Weight(None, w1, R)
    weight_2 = Weight(w2_in.at[rows_of(me, R)], w2, R)
    own_cot = load(cot_in, cotb.at[me])

    own_small.wait()
    for copy in small_copies:
        copy.wait_recv()
    for row in range(7):
        vec[row : row + 1, :] = jnp.concatenate(
            [smb[s, row : row + 1, :R] for s in range(F)], axis=1
        )
    groups = 3 * D // R // 3
    heads = []
    for t in range(3):
        start = t * groups + me * (hw // R)
        line = jnp.concatenate(
            [
                smb[(start + b) // 3, pl.ds(7 + (start + b) % 3, 1), :][:, :R]
                for b in range(hw // R)
            ],
            axis=1,
        )
        for h in range(hl):
            heads.append(lane_pad(line[:, h * HD : (h + 1) * HD], W))
    bqkv[...] = jnp.broadcast_to(jnp.concatenate(heads, axis=1), bqkv.shape)

    def vector(row):
        return vec[row : row + 1, :]

    own_plc.wait()
    for c1, _ in tok_copies:
        c1.wait_recv()

    def table(i, carry):
        rows = rows_of(i, T)
        turned = jnp.transpose(plb[i], (1, 0))
        plt[rows, :] = turned
        angle = turned[:, 1:2] * wave_in[0:1, :] + turned[:, 2:3] * wave_in[1:2, :]
        cosb[rows, :] = jnp.cos(angle)
        sinb[rows, :] = jnp.sin(angle) * wave_in[2:3, :]
        return carry

    lax.fori_loop(0, n, table, 0)
    lane = lax.broadcasted_iota(jnp.int32, (1, W), 1)
    low_half = lane < HD // 2

    def swap(value):
        return jnp.where(
            low_half, pltpu.roll(value, W - HD // 2, 1), pltpu.roll(value, HD // 2, 1)
        )

    def norm_one(i):
        def body(rows):
            normed, _ = moments(tokb[i, rows, :].astype(F32))
            ain[rows_of_block(i, rows), :] = (normed * vector(0) + vector(1)).astype(BF)

        strips(T, strip, body)

    def rows_of_block(i, rows):
        return pl.ds(pl.multiple_of(i * T + rows.start, strip), strip)

    own_tok.wait()
    norm_one(me)
    for o in range(1, n):
        tok_copies[o - 1][1].wait_recv()
        norm_one(seq_from[o])

    weight_q.relay()
    weight_q.finish()

    def spread_heads(rows):
        line = wqc[rows, :]
        for h in range(3 * hl):
            wq[rows, h * W : (h + 1) * W] = lane_pad(line[:, h * HD : (h + 1) * HD], W)

    strips(D, R, spread_heads)

    def project(i, carry):
        rows = rows_of(i, T)
        line = ain[rows, :]
        cosine = cosb[rows, :]
        sine = sinb[rows, :]
        for t in range(3):
            part = mm(line, wq[:, t * QW : (t + 1) * QW]) + bqkv[0:1, t * QW : (t + 1) * QW]
            for h in range(hl):
                u = part[:, h * W : (h + 1) * W]
                if t < 2:
                    u = u * cosine + swap(u) * sine
                qkv[rows, t * QW + h * W : t * QW + (h + 1) * W] = u.astype(BF)
        return carry

    lax.fori_loop(0, n, project, 0)

    def masked(scores, i):
        ids = jnp.concatenate([plb[b, 3:4, :] for b in range(n)], axis=1)
        own_ids = plt[rows_of(i, T), 3:4]
        return jnp.where(own_ids == ids, scores * scale, MASKED)

    mix_send, mix_recv = take(n * (n - 1)), take(n * (n - 1))

    def mix_copy(i, o, peer, source):
        return pltpu.make_async_remote_copy(
            src_ref=mixc.at[source, i],
            dst_ref=mixc.at[source, i],
            send_sem=sems.at[mix_send + i * (n - 1) + o - 1],
            recv_sem=sems.at[mix_recv + i * (n - 1) + o - 1],
            device_id={"seq": peer},
            device_id_type=MESH,
        )

    def attend_block(i, carry):
        rows = rows_of(i, T)
        outs = []
        logs = jnp.zeros((T, W), F32)
        for h in range(hl):
            q = qkv[rows, h * W : (h + 1) * W]
            kk = qkv[:, QW + h * W : QW + (h + 1) * W]
            v = qkv[:, 2 * QW + h * W : 2 * QW + (h + 1) * W]
            s = masked(mm_nt(q, kk), i)
            top = jnp.max(s, axis=-1, keepdims=True)
            p = jnp.exp(s - top)
            total = jnp.sum(p, axis=-1, keepdims=True)
            outs.append((mm(p.astype(BF), v) / total)[:, :HD].astype(BF))
            logs = jnp.where(lane == h, top + jnp.log(total), logs)
        lse[rows, :] = logs
        mixc[me, i] = lane_pad(jnp.concatenate(outs, axis=1), HP)
        for o in range(1, n):
            mix_copy(i, o, seq_to[o], me).start()
        return carry

    lax.fori_loop(0, n, attend_block, 0)
    cot_copies = [
        send(cot_in, cotb.at[me], {"seq": seq_to[o]}, take()) for o in range(1, n)
    ]

    weight_p.relay()
    weight_p.finish()

    def branch(t, carry):
        i = (me + 1 + t) % n
        rows = rows_of(i, T)
        for o in range(1, n):
            mix_copy(i, o, seq_to[o], seq_from[o]).wait_recv()
        mix[rows, :] = jnp.concatenate([mixc[c, i][:, :hw] for c in range(n)], axis=1)
        mid[...] = mm(mix[rows, :], wp[...])

        def body(part):
            whole = rows_of_block(i, part)
            value = mid[part, :] + tokb[i, part, :].astype(F32) + vector(2)
            mid[part, :] = value
            normed, _ = moments(value)
            mlp[whole, :] = (normed * vector(3) + vector(4)).astype(BF)

        strips(T, strip, body)
        return carry

    lax.fori_loop(0, n, branch, 0)

    weight_1.relay()
    weight_1.finish()

    def up(i, carry):
        rows = rows_of(i, T)
        before = mm(mlp[rows, :], w1[...]) + vector(6)
        gate = jax.nn.sigmoid(1.702 * before)
        act[rows, :] = (before * gate).astype(BF)
        dge[rows, :] = (gate + 1.702 * before * gate * (1.0 - gate)).astype(BF)
        return carry

    lax.fori_loop(0, n, up, 0)

    own_cot.wait()
    for copy in cot_copies:
        copy.wait_recv()
    weight_2.relay()
    weight_2.finish()

    class Scatter:
        def __init__(self, stage):
            self.stage = stage
            self.out, self.into = take(n - 1), take(n - 1)

        def copy(self, t, to):
            return pltpu.make_async_remote_copy(
                src_ref=band(self.stage, to, T),
                dst_ref=rsr.at[t],
                send_sem=sems.at[self.out + t],
                recv_sem=sems.at[self.into + t],
                device_id={"seq": to},
                device_id_type=MESH,
            )

        def start(self, t, i):
            @pl.when(t < n - 1)
            def _():
                self.copy(t, i).start()

        def wait_recv(self):
            for t in range(n - 1):
                self.copy(t, seq_to[t + 1]).wait_recv()

        def wait_send(self):
            for t in range(n - 1):
                self.copy(t, seq_to[t + 1]).wait_send()

    for i in range(n):
        for o in range(1, n):
            mix_copy(i, o, seq_to[o], me).wait_send()
    scatter_mlp = Scatter(snd)

    def back(t, carry):
        i = (me + 1 + t) % n
        rows = rows_of(i, T)
        grad = (mm_nt(cotb[i], w2[...]) * dge[rows, :].astype(F32)).astype(BF)
        dge[rows, :] = grad
        snd[rows, :] = mm_nt(grad, w1[...]).astype(BF)
        scatter_mlp.start(t, i)
        return carry

    lax.fori_loop(0, n, back, 0)

    class Gradient:
        def __init__(self, grad, other, far, result, lanes):
            self.grad, self.other, self.far, self.result = grad, other, far, result
            self.lanes = lanes

        def exchange(self):
            self.near = []
            for c in range(J):
                self.near.append(
                    send(
                        band(self.grad, 2 * c + 1 - k, R),
                        self.other.at[c],
                        {"fsdp": partner},
                        take(),
                    )
                )

        def add_near(self):
            for copy in self.near:
                copy.wait_recv()

            def chip(c, carry):
                rows = rows_of(2 * c + k, R)
                self.grad[rows, :] = (
                    self.grad[rows, :].astype(F32) + self.other[c].astype(F32)
                ).astype(BF)
                return carry

            lax.fori_loop(0, J, chip, 0)
            self.across = [
                send(
                    band(self.grad, z_to[d], R),
                    self.far.at[d - 1],
                    {"fsdp": z_to[d]},
                    take(),
                )
                for d in range(1, J)
            ]

        def add_far(self):
            for copy in self.across:
                copy.wait_recv()
            rows = rows_of(f, R)
            total = self.grad[rows, :].astype(F32)
            for d in range(J - 1):
                total = total + self.far[d].astype(F32)
            self.other[0] = total.astype(BF)
            mine = self.other.at[0]
            self.keep = load(mine, self.result.at[me])
            self.share = [
                send(mine, self.result.at[me], {"seq": seq_to[o]}, take()) for o in range(1, n)
            ]

        def finish(self):
            self.keep.wait()
            for copy in self.share:
                copy.wait_recv()

    grad_up = Gradient(w1, d14, z13, r1_ref, P1)
    grad_down = Gradient(w2, d24, z23, r2_ref, D)
    grad_proj = Gradient(gp, dp4, zp3, rp_ref, HP)
    grad_qkv = Gradient(wqc, dq4, zq3, rq_ref, CQ)

    weight_1.drain()
    weight_2.drain()
    weight_q.drain()

    def up_grad(t, carry):
        w1[rows_of(t, tile), :] = mm_tn(mlp[:, rows_of(t, tile)], dge[...]).astype(BF)
        return carry

    lax.fori_loop(0, D // tile, up_grad, 0)
    grad_up.exchange()

    def down(i, carry):
        rows = rows_of(i, T)
        mlp[rows, :] = mm(act[rows, :], w2[...]).astype(BF)
        return carry

    lax.fori_loop(0, n, down, 0)

    def down_grad(t, carry):
        lanes = rows_of(t, tile)
        total = mm_tn(act[0:T, lanes], cotb[0])
        for b in range(1, n):
            total = total + mm_tn(act[b * T : (b + 1) * T, lanes], cotb[b])
        w2[lanes, :] = total.astype(BF)
        return carry

    lax.fori_loop(0, P1 // tile, down_grad, 0)
    grad_down.exchange()

    smg[...] = jnp.zeros(smg.shape, F32)
    scatter_mlp.wait_recv()

    def gather_parts(part):
        whole = rows_of_block(me, part)
        total = snd[whole, :].astype(F32)
        for t in range(n - 1):
            total = total + rsr[t, part, :].astype(F32)
        return total

    def add_sum(row, value):
        smg[row : row + 1, :] = smg[row : row + 1, :] + jnp.sum(value, axis=0, keepdims=True)

    def norm_two_back(part):
        upstream = cotb[me, part, :].astype(F32)
        grad = gather_parts(part)
        normed, factor = moments(mid[part, :])
        scaled = grad * vector(3)
        value = upstream + factor * (
            scaled
            - jnp.mean(scaled, axis=-1, keepdims=True)
            - normed * jnp.mean(scaled * normed, axis=-1, keepdims=True)
        )
        gmd[part, :] = value
        low = value.astype(BF)
        snd[rows_of_block(me, part), :] = low
        add_sum(2, low.astype(F32))
        add_sum(3, grad * normed)
        add_sum(4, grad)
        add_sum(5, upstream)

    strips(T, strip, norm_two_back)
    own_rows = rows_of(me, T)
    low_branch = snd[own_rows, :]
    grad_mixed = mm_nt(low_branch, wp[...]).astype(BF)
    for c in range(n):
        mixc[0, c] = lane_pad(grad_mixed[:, c * hw : (c + 1) * hw], HP)
        mixc[2, c] = lane_pad(low_branch[:, c * hw : (c + 1) * hw], HP)
    head_copies = [
        send(mixc.at[0, seq_to[o]], mixc.at[1, me], {"seq": seq_to[o]}, take()) for o in range(1, n)
    ]
    branch_copies = [
        send(mixc.at[2, seq_to[o]], mixc.at[3, me], {"seq": seq_to[o]}, take()) for o in range(1, n)
    ]
    mixc[1, me] = mixc[0, me]
    mixc[3, me] = mixc[2, me]

    grad_up.add_near()
    grad_down.add_near()

    for copy in head_copies:
        copy.wait_recv()
    out_copies = [
        send(band(mlp, seq_to[o], T), tokb.at[me], {"seq": seq_to[o]}, take()) for o in range(1, n)
    ]

    for h in range(hl):
        q_at = slice(h * W, (h + 1) * W)
        k_at = slice(QW + h * W, QW + (h + 1) * W)
        v_at = slice(2 * QW + h * W, 2 * QW + (h + 1) * W)
        dkv[...] = jnp.zeros(dkv.shape, F32)

        def attend_back_block(i, carry):
            rows = rows_of(i, T)
            q = qkv[rows, q_at]
            kk = qkv[:, k_at]
            g = lane_pad(mixc[1, i][:, h * HD : (h + 1) * HD], W)
            p = jnp.exp(masked(mm_nt(q, kk), i) - lse[rows, h : h + 1])
            dp = mm_nt(g, qkv[:, v_at])
            dkv[:, W:] = dkv[:, W:] + mm_tn(p.astype(BF), g)
            centre = jnp.sum(p * dp, axis=-1, keepdims=True)
            ds = (p * (dp - centre)).astype(BF)
            dq = (mm(ds, kk) * scale).astype(BF).astype(F32)
            dkv[:, :W] = dkv[:, :W] + mm_tn(ds, q)
            qkv[rows, q_at] = (dq * cosb[rows, :] - swap(dq) * sinb[rows, :]).astype(BF)
            return carry

        lax.fori_loop(0, n, attend_back_block, 0)

        def turn_back(i, carry):
            rows = rows_of(i, T)
            dk = (dkv[rows, :W] * scale).astype(BF).astype(F32)
            qkv[rows, k_at] = (dk * cosb[rows, :] - swap(dk) * sinb[rows, :]).astype(BF)
            qkv[rows, v_at] = dkv[rows, W:].astype(BF)
            return carry

        lax.fori_loop(0, n, turn_back, 0)

    scatter_mlp.wait_send()
    scatter_attn = Scatter(snd)

    def attn_back(t, carry):
        i = (me + 1 + t) % n
        rows = rows_of(i, T)
        snd[rows, :] = mm_nt(qkv[rows, :], wq[...]).astype(BF)
        scatter_attn.start(t, i)
        return carry

    lax.fori_loop(0, n, attn_back, 0)

    def qkv_grad(t, carry):
        rows = rows_of(t, tile)
        total = mm_tn(ain[:, rows], qkv[...])
        wqc[rows, :] = lane_pad(
            jnp.concatenate([total[:, h * W : h * W + HD].astype(BF) for h in range(3 * hl)], axis=1),
            CQ,
        )
        return carry

    lax.fori_loop(0, D // tile, qkv_grad, 0)
    grad_qkv.exchange()

    for copy in branch_copies:
        copy.wait_recv()

    def proj_grad(t, carry):
        lanes = rows_of(t, tile)
        total = mm_tn(mix[0:T, lanes], mixc[3, 0])
        for b in range(1, n):
            total = total + mm_tn(mix[b * T : (b + 1) * T, lanes], mixc[3, b])
        gp[lanes, :] = total.astype(BF)
        return carry

    lax.fori_loop(0, D // tile, proj_grad, 0)
    grad_proj.exchange()
    grad_qkv.add_near()
    grad_proj.add_near()
    grad_up.add_far()
    grad_down.add_far()

    def bias_sums(part):
        smg[6:7, :] = smg[6:7, :] + jnp.sum(dge[part, :].astype(F32), axis=0, keepdims=True)
        line = jnp.sum(qkv[part, :].astype(F32), axis=0, keepdims=True)
        line = lane_pad(
            jnp.concatenate([line[:, h * W : h * W + HD] for h in range(3 * hl)], axis=1), D
        )
        smg[7:8, :] = smg[7:8, :] + line

    strips(L, 64, bias_sums)

    scatter_attn.wait_recv()

    def norm_one_back(part):
        grad = gather_parts(part)
        normed, factor = moments(tokb[me, part, :].astype(F32))
        scaled = grad * vector(0)
        gmd[part, :] = gmd[part, :] + factor * (
            scaled
            - jnp.mean(scaled, axis=-1, keepdims=True)
            - normed * jnp.mean(scaled * normed, axis=-1, keepdims=True)
        )
        add_sum(0, grad * normed)
        add_sum(1, grad)

    strips(T, strip, norm_one_back)
    tokens_out = load(gmd, tgrad_ref)
    sum_copies = [
        send(smg, sg8.at[f], {"fsdp": (f + o) % F}, take()) for o in range(1, F)
    ]
    sg8[f] = smg[...]

    for copy in out_copies:
        copy.wait_recv()

    def write_out(part):
        whole = rows_of_block(me, part)
        total = mid[part, :] + mlp[whole, :].astype(F32) + vector(5)
        for o in range(1, n):
            total = total + tokb[seq_from[o], part, :].astype(F32)
        bias_rows = rows_of_block(me, part)
        ain[bias_rows, :] = total.astype(BF)

    strips(T, strip, write_out)
    block_out = load(band(ain, me, T), out_ref)

    for copy in sum_copies:
        copy.wait_recv()
    total = sg8[0]
    for s in range(1, F):
        total = total + sg8[s]
    plain = lax.broadcasted_iota(jnp.int32, total.shape, 0)
    vec[...] = jnp.where(plain < 8, total, 0.0)
    sums_keep = load(vec, sums_ref.at[me])
    sums_share = [
        send(vec, sums_ref.at[me], {"seq": seq_to[o]}, take()) for o in range(1, n)
    ]

    grad_qkv.add_far()
    grad_proj.add_far()
    for item in (grad_up, grad_down, grad_proj, grad_qkv):
        item.finish()
    for copy in sums_share:
        copy.wait_recv()
    sums_keep.wait()
    tokens_out.wait()
    block_out.wait()
    weight_p.drain()
    scatter_attn.wait_send()
    for copy in leftover:
        copy.wait_send()


def unpack_kernel(
    dims,
    block_in,
    tokens_in,
    rq_in,
    rp_in,
    r1_in,
    r2_in,
    sums_in,
    block_ref,
    tokens_ref,
    qkv_ref,
    proj_ref,
    up_ref,
    down_ref,
    vec_ref,
    block,
    tokens,
    rq,
    rp,
    r1,
    r2,
    sums,
    stage,
    vec,
    in_sems,
    out_sems,
):
    n, T, L, D, F, R, hl, P1, CQ, HP = dims
    hw = hl * HD
    f = lax.axis_index("fsdp")
    loads = []
    for src, dst in (
        (r2_in, r2),
        (r1_in, r1),
        (rq_in, rq),
        (rp_in, rp),
        (tokens_in, tokens),
        (block_in, block),
        (sums_in, sums),
    ):
        copy = pltpu.make_async_copy(src, dst, in_sems.at[len(loads)])
        copy.start()
        loads.append(copy)
    stores = []

    def store(src, dst):
        copy = pltpu.make_async_copy(src, dst, out_sems.at[len(stores)])
        copy.start()
        stores.append(copy)

    loads[0].wait()
    for c in range(n):
        stage[c] = r2[c].astype(F32)
        store(stage.at[c], down_ref.at[c * R : (c + 1) * R])
    loads[1].wait()
    width = n * R
    for c in range(n):
        blocks = range(c * P1 // width, (c + 1) * P1 // width)
        stage[n + c] = jnp.concatenate(
            [r1[m, :, b * R : (b + 1) * R] for b in blocks for m in range(n)], axis=1
        ).astype(F32)
        store(stage.at[n + c], up_ref.at[:, c * P1 : (c + 1) * P1])
    loads[2].wait()
    for t in range(3):
        stage[2 * n + t] = jnp.concatenate(
            [rq[m, :, t * hw : (t + 1) * hw] for m in range(n)], axis=1
        ).astype(F32)
        store(stage.at[2 * n + t], qkv_ref.at[:, t * D : (t + 1) * D])
    loads[3].wait()
    stage[2 * n + 3] = jnp.concatenate([rp[m, :, :hw] for m in range(n)], axis=1).astype(F32)
    store(stage.at[2 * n + 3], proj_ref)
    loads[4].wait()
    store(tokens, tokens_ref)
    loads[5].wait()
    store(block, block_ref)
    loads[6].wait()
    per_part = hw // R
    for s in range(F):

        @pl.when(f == s)
        def _():
            own = slice(s * R, (s + 1) * R)
            total = sums[0, 0:6, own]
            for m in range(1, n):
                total = total + sums[m, 0:6, own]
            lines = [total] + [sums[m, 6:7, own] for m in range(n)]
            for b in range(3):
                spot = 3 * s + b
                third, rest = spot // (n * per_part), spot % (n * per_part)
                at = third * hw + rest % per_part * R
                lines.append(sums[rest // per_part, 7:8, at : at + R])
            lines.append(jnp.zeros((16 - 9 - n, R), F32))
            vec[...] = jnp.concatenate(lines, axis=0)

    store(vec, vec_ref)
    for copy in stores:
        copy.wait()


def round_up(value, step):
    return -(-value // step) * step


def shards_kernel(
    tokens,
    picture_ids,
    patch_rows,
    patch_cols,
    norm1_gain,
    norm1_bias,
    qkv_weight,
    qkv_bias,
    proj_weight,
    proj_bias,
    norm2_gain,
    norm2_bias,
    fc1_weight,
    fc1_bias,
    fc2_weight,
    fc2_bias,
    cotangent,
):
    n = lax.axis_size("seq")
    me = lax.axis_index("seq")
    F = lax.axis_size("fsdp")
    f = lax.axis_index("fsdp")
    _, T, D = tokens.shape
    L = n * T
    hl = D // HD // n
    hw = hl * HD
    R = D // F
    hidden = fc1_weight.shape[1]
    P1 = hidden // n
    part = hidden // (F * n)
    CQ = round_up(3 * hw, 128)
    HP = round_up(hw, 128)
    J = F // 2
    W = 128

    def pick(value, axis):
        return lax.dynamic_index_in_dim(value, me, axis, keepdims=False)

    small = jnp.concatenate(
        [
            norm1_gain,
            norm1_bias,
            proj_bias,
            norm2_gain,
            norm2_bias,
            fc2_bias,
            pick(fc1_bias.reshape(n, part), 0),
            qkv_bias,
        ]
    )
    small = jnp.pad(small.astype(F32).reshape(10, R), ((0, 6), (0, 0)))
    spot = jnp.arange(T, dtype=jnp.int32) + me * T
    ids = jnp.where(picture_ids[0] >= 0, picture_ids[0], -1 - spot)
    places = jnp.stack([picture_ids[0], patch_rows[0], patch_cols[0], ids]).astype(F32)
    places = jnp.pad(places, ((0, 4), (0, 0)))
    quarter = HD // 4
    inverse = 10000.0 ** (-np.arange(quarter) / quarter)
    wave = np.zeros((8, W), np.float32)
    for c in range(2):
        wave[0, 2 * c * quarter : (2 * c + 1) * quarter] = inverse
        wave[1, (2 * c + 1) * quarter : (2 * c + 2) * quarter] = inverse
    wave[2] = np.where(np.arange(W) < HD // 2, -1.0, 1.0)
    dims = (n, T, L, D, F, R, hl, P1, CQ, HP)
    anywhere = pl.BlockSpec(memory_space=pl.ANY)
    local = pl.BlockSpec(memory_space=pltpu.VMEM)

    def vmem(shape, dtype=BF):
        return pltpu.VMEM(shape, dtype)

    scratch = [
        vmem((n, T, D)),
        vmem((L, D)),
        vmem((n, T, D)),
        vmem((n, 8, T), F32),
        vmem((L, 8), F32),
        vmem((F, 16, R), F32),
        vmem((8, D), F32),
        vmem((8, 3 * hl * W), F32),
        vmem((L, W), F32),
        vmem((L, W), F32),
        vmem((D, CQ)),
        vmem((D, 3 * hl * W)),
        vmem((D, D)),
        vmem((D, P1)),
        vmem((P1, D)),
        vmem((L, 3 * hl * W)),
        vmem((L, W), F32),
        vmem((n, n, T, HP)),
        vmem((L, D)),
        vmem((T, D), F32),
        vmem((L, D)),
        vmem((L, P1)),
        vmem((L, P1)),
        vmem((L, D)),
        vmem((n - 1, T, D)),
        vmem((T, D), F32),
        vmem((D, HP)),
        vmem((J, R, CQ)),
        vmem((J, R, HP)),
        vmem((J, R, P1)),
        vmem((J, R, D)),
        vmem((J - 1, R, CQ)),
        vmem((J - 1, R, HP)),
        vmem((J - 1, R, P1)),
        vmem((J - 1, R, D)),
        vmem((L, 2 * W), F32),
        vmem((8, D), F32),
        vmem((F, 8, D), F32),
        pltpu.SemaphoreType.DMA((320,)),
        pltpu.SemaphoreType.DMA((24,)),
    ]
    shapes = (
        jax.ShapeDtypeStruct((T, D), BF),
        jax.ShapeDtypeStruct((T, D), F32),
        jax.ShapeDtypeStruct((n, R, CQ), BF),
        jax.ShapeDtypeStruct((n, R, HP), BF),
        jax.ShapeDtypeStruct((n, R, P1), BF),
        jax.ShapeDtypeStruct((n, R, D), BF),
        jax.ShapeDtypeStruct((n, 8, D), F32),
    )
    block_out, tokens_grad, rq, rp, r1, r2, sums = pl.pallas_call(
        functools.partial(block_kernel, dims),
        out_shape=shapes,
        in_specs=[anywhere] * 4 + [local] + [anywhere] * 4,
        out_specs=[anywhere] * 7,
        scratch_shapes=scratch,
        compiler_params=pltpu.CompilerParams(
            collective_id=0, has_side_effects=True, vmem_limit_bytes=67043328
        ),
    )(tokens[0], cotangent[0], places, small, wave, qkv_weight, proj_weight, fc1_weight, fc2_weight)
    stored = (
        jax.ShapeDtypeStruct((T, D), BF),
        jax.ShapeDtypeStruct((T, D), F32),
        jax.ShapeDtypeStruct((R, 3 * D), F32),
        jax.ShapeDtypeStruct((R, D), F32),
        jax.ShapeDtypeStruct((R, hidden), F32),
        jax.ShapeDtypeStruct((n * R, D), F32),
        jax.ShapeDtypeStruct((16, R), F32),
    )
    block_out, tokens_grad, full_qkv, full_proj, full_up, full_down, sums = pl.pallas_call(
        functools.partial(unpack_kernel, dims),
        out_shape=stored,
        in_specs=[anywhere] * 7,
        out_specs=[anywhere] * 7,
        scratch_shapes=[
            vmem((T, D)),
            vmem((T, D), F32),
            vmem((n, R, CQ)),
            vmem((n, R, HP)),
            vmem((n, R, P1)),
            vmem((n, R, D)),
            vmem((n, 8, D), F32),
            vmem((4 + 2 * n, R, D), F32),
            vmem((16, R), F32),
            pltpu.SemaphoreType.DMA((7,)),
            pltpu.SemaphoreType.DMA((7 + 2 * n,)),
        ],
        compiler_params=pltpu.CompilerParams(vmem_limit_bytes=40000000),
    )(block_out, tokens_grad, rq, rp, r1, r2, sums)
    return (
        block_out[None],
        tokens_grad[None],
        sums[0],
        sums[1],
        full_qkv,
        sums[6 + n : 9 + n].reshape(3 * R),
        full_proj,
        sums[2],
        sums[3],
        sums[4],
        full_up,
        sums[6 : 6 + n].reshape(n * R),
        full_down,
        sums[5],
    )


def fits_kernel(mesh):
    return dict(mesh.shape) == {"seq": 4, "fsdp": 8}


def shards_plain(
    tokens,
    picture_ids,
    patch_rows,
    patch_cols,
    norm1_gain,
    norm1_bias,
    qkv_weight,
    qkv_bias,
    proj_weight,
    proj_bias,
    norm2_gain,
    norm2_bias,
    fc1_weight,
    fc1_bias,
    fc2_weight,
    fc2_bias,
    cotangent,
):
    n = lax.axis_size("seq")
    me = lax.axis_index("seq")
    stores = lax.axis_size("fsdp")
    _, own, width = tokens.shape
    heads = width // HD
    local_heads = heads // n
    hw = local_heads * HD
    rows = qkv_weight.shape[0]
    hidden = fc1_weight.shape[1]
    part = hidden // (stores * n)

    def pick(value, axis):
        return lax.dynamic_index_in_dim(value, me, axis, keepdims=False)

    own_qkv = pick(qkv_weight.reshape(rows, 3, n, hw), 2).reshape(rows, 3 * hw)
    own_up = pick(fc1_weight.reshape(rows, stores, n, part), 2).reshape(rows, stores * part)
    own_down = pick(fc2_weight.reshape(n, part, width), 0)
    small = (norm1_gain, norm1_bias, proj_bias, norm2_gain, norm2_bias, fc2_bias, qkv_bias, fc1_bias)
    sizes = [item.shape[0] for item in small]
    packed = gather(jnp.concatenate(small)[None], "fsdp")
    weight_qkv = gather(own_qkv, "fsdp")
    weight_proj = gather(proj_weight, "fsdp")
    weight_up = gather(own_up, "fsdp")
    weight_down = gather(own_down, "fsdp")
    params = []
    start = 0
    for size in sizes:
        params.append(packed[:, start : start + size].reshape(-1).astype(F32))
        start += size
    gain_one, bias_one, bias_proj, gain_two, bias_two, bias_down, bias_qkv, bias_up = params
    bias_qkv = pick(bias_qkv.reshape(3, n, hw), 1).reshape(3 * hw)
    bias_up = pick(bias_up.reshape(stores, n, part), 1).reshape(stores * part)

    places = jnp.stack([picture_ids[0], patch_rows[0], patch_cols[0]])
    places = gather(places, "seq", 1)
    picture = places[0]
    all_tokens = gather(tokens[0], "seq").astype(F32)
    upstream = gather(cotangent[0], "seq")
    length = all_tokens.shape[0]

    def mine(value):
        return lax.dynamic_slice_in_dim(value, me * own, own, 0)

    normed_one, factor_one = standardize(all_tokens)
    attn_input = (normed_one * gain_one + bias_one).astype(BF)
    projected = (dot(attn_input, weight_qkv) + bias_qkv).reshape(length, 3, local_heads, HD)
    cosine, sine = rotary_tables(places[1], places[2], HD)
    queries = rotate(projected[:, 0], cosine, sine).astype(BF)
    keys = rotate(projected[:, 1], cosine, sine).astype(BF)
    values = projected[:, 2].astype(BF)
    mixed_own, log_total = attend(queries, keys, values, picture)
    mixed = gather(mixed_own.reshape(length, hw), "seq", 1)
    middle = all_tokens + dot(mixed, weight_proj) + bias_proj
    normed_two, factor_two = standardize(middle)
    mlp_input = (normed_two * gain_two + bias_two).astype(BF)
    before = dot(mlp_input, weight_up) + bias_up
    gate = jax.nn.sigmoid(1.702 * before)
    activated = (before * gate).astype(BF)
    out_part = dot(activated, weight_down).astype(BF)
    block_out = (mine(middle) + scatter_sum(out_part, "seq").astype(F32) + bias_down).astype(BF)

    grad_down = scatter_sum(rows_term(activated, upstream).astype(BF), "fsdp")
    grad_activated = contract_back(upstream, weight_down)
    grad_before = (grad_activated * (gate + 1.702 * before * gate * (1.0 - gate))).astype(BF)
    grad_up = scatter_sum(rows_term(mlp_input, grad_before).astype(BF), "fsdp")
    grad_mlp_input = scatter_sum(contract_back(grad_before, weight_up).astype(BF), "seq").astype(F32)
    own_upstream = cotangent[0].astype(F32)
    own_two = mine(normed_two)
    grad_middle = own_upstream + norm_back(grad_mlp_input, own_two, mine(factor_two), gain_two)
    grad_branch = grad_middle.astype(BF)
    grad_mixed = contract_back(grad_branch, weight_proj).astype(BF)
    grad_heads = lax.all_to_all(grad_mixed, "seq", split_axis=1, concat_axis=0, tiled=True)
    branch_part = lax.all_to_all(grad_branch, "seq", split_axis=1, concat_axis=0, tiled=True)
    grad_proj = scatter_sum(rows_term(mixed, branch_part).astype(BF), "fsdp")
    grad_queries, grad_keys, grad_values = attend_back(
        queries, keys, values, picture, grad_heads.reshape(length, local_heads, HD), log_total
    )
    grad_projected = jnp.stack(
        [
            unrotate(grad_queries.astype(F32), cosine, sine).astype(BF),
            unrotate(grad_keys.astype(F32), cosine, sine).astype(BF),
            grad_values,
        ],
        axis=1,
    ).reshape(length, 3 * hw)
    grad_qkv = scatter_sum(rows_term(attn_input, grad_projected).astype(BF), "fsdp")
    grad_attn_input = scatter_sum(contract_back(grad_projected, weight_qkv).astype(BF), "seq").astype(F32)
    own_one = mine(normed_one)
    tokens_grad = grad_middle + norm_back(grad_attn_input, own_one, mine(factor_one), gain_one)

    def spread(value, groups):
        empty = jnp.zeros((groups, n, value.shape[0] // groups), F32)
        return lax.dynamic_update_slice_in_dim(
            empty, value.reshape(groups, 1, -1), me, 1
        ).reshape(stores, -1)

    sums = [
        jnp.sum(grad_attn_input * own_one, axis=0).reshape(stores, -1),
        jnp.sum(grad_attn_input, axis=0).reshape(stores, -1),
        jnp.sum(grad_branch.astype(F32), axis=0).reshape(stores, -1),
        jnp.sum(grad_mlp_input * own_two, axis=0).reshape(stores, -1),
        jnp.sum(grad_mlp_input, axis=0).reshape(stores, -1),
        jnp.sum(own_upstream, axis=0).reshape(stores, -1),
        spread(jnp.sum(grad_projected.astype(F32), axis=0), 3),
        spread(jnp.sum(grad_before.astype(F32), axis=0), stores),
    ]
    summed = lax.psum(scatter_sum(jnp.concatenate(sums, axis=1), "fsdp"), "seq")[0]
    finals = []
    start = 0
    for size in sizes:
        finals.append(summed[start : start + size])
        start += size
    full_down = gather(grad_down, "seq").astype(F32)
    full_up = gather(grad_up[None], "seq").reshape(n, rows, stores, part)
    full_up = full_up.transpose(1, 2, 0, 3).reshape(rows, hidden).astype(F32)
    full_proj = gather(grad_proj, "seq", 1).astype(F32)
    full_qkv = gather(grad_qkv[None], "seq").reshape(n, rows, 3, hw)
    full_qkv = full_qkv.transpose(1, 2, 0, 3).reshape(rows, 3 * width).astype(F32)
    return (
        block_out[None],
        tokens_grad[None],
        finals[0],
        finals[1],
        full_qkv,
        finals[6],
        full_proj,
        finals[2],
        finals[3],
        finals[4],
        full_up,
        finals[7],
        full_down,
        finals[5],
    )


def solution(mesh):
    token = P("fsdp", "seq", None)
    place = P("fsdp", "seq")
    vector = P("fsdp")
    matrix = P("fsdp", None)
    in_specs = (
        token,
        place,
        place,
        place,
        vector,
        vector,
        matrix,
        vector,
        matrix,
        vector,
        vector,
        vector,
        matrix,
        vector,
        matrix,
        vector,
        token,
    )
    out_specs = (
        token,
        token,
        vector,
        vector,
        matrix,
        vector,
        matrix,
        vector,
        vector,
        vector,
        matrix,
        vector,
        matrix,
        vector,
    )
    shards = shards_kernel if fits_kernel(mesh) else shards_plain
    return jax.shard_map(shards, mesh=mesh, in_specs=in_specs, out_specs=out_specs, check_vma=False)
```

profile of v0, /device:TPU:16, one launch (start us, length us, event | category | flops | bytes accessed | tf_op | source)
XLA Modules:
  0.0 350.0 jit_solution(17382502668314265039)
XLA Ops:
  0.7 0.7 compare_select_fusion
  1.3 0.8 reshape.51
  2.1 0.7 add_convert_fusion
  2.9 4.8 %concatenate.3 = bf16[1600]{0:T(1024)(128)(2,1)S(1)} concatenate(bf16[160]{0:T(256)(128)(2,1)} %param.22, bf16[160]{0:T(256)(128)(2,1)} %param.23, bf16[160]{0:T(256)(128)(2,1)} %param.27, bf16[160]{0:T(256)(128)(2,1)} %param.28, bf16[160]{0:T(256)(128)(2,1)} %param.29, bf16[160]{0:T(256)(128)(2,1)} %param.33, bf16[160]{0:T(256)(128)(2,1)S(1)} %dynamic-slice_reduce_fusion, ...), dimensions={0} | concatenate | bytes 6400 | tf_op jit(solution)/shard_map/concatenate | solution.py:996
  7.6 0.1 convert_element_type.13
  7.7 0.6 pad.10.plc_in
  8.3 0.6 pad_convert_fusion.small_in
  9.0 324.7 %shard_map.281 = (bf16[256,1280]{1,0:T(8,128)(2,1)}, f32[256,1280]{1,0:T(8,128)}, bf16[4,160,1024]{2,1,0:T(8,128)(2,1)}, bf16[4,160,384]{2,1,0:T(8,128)(2,1)}, b...) custom-call(bf16[256,1280]{1,0:T(8,128)(2,1)} %bitcast.10, ...), custom_call_target="tpu_custom_call" | custom-call | tf_op jit(solution)/shard_map/pallas_call | solution.py:1078
  333.7 0.0 copy-start
  333.7 1.4 copy-done
  335.1 0.0 copy-start.1
  335.1 1.4 copy-done.1
  336.6 0.0 copy-start.2
  336.6 1.3 copy-done.2
  337.9 0.0 copy-start.3
  337.9 1.3 copy-done.3
  339.2 0.0 copy-start.4
  339.2 1.1 copy-done.4
  340.3 0.0 copy-start.5
  340.3 1.0 copy-done.5
  341.3 0.0 copy-start.6
  341.3 0.9 copy-done.6
  342.2 5.9 %shard_map.282 = (bf16[256,1280]{1,0:T(8,128)(2,1)}, f32[256,1280]{1,0:T(8,128)}, f32[160,3840]{1,0:T(8,128)}, f32[160,1280]{1,0:T(8,128)}, f32[160,5120]{1,0:T(...) custom-call(bf16[256,1280]{1,0:T(8,128)(2,1)S(1)} %copy-done.4, f32[256,1280]{1,0:T(8,128)S(1)} %copy-done.2, ...), custom_call_target="tpu_custom_call" | custom-call | tf_op jit(solution)/shard_map/pallas_call | solution.py:1097
  348.1 0.7 reshape.52
  348.8 0.6 fusion
  349.4 0.7 reshape.53
  (3 shorter events, 0.0 us)
Async XLA Ops:
  333.7 1.4 copy-start
  335.1 1.4 copy-start.1
  336.6 1.3 copy-start.2
  337.9 1.3 copy-start.3
  339.2 1.1 copy-start.4
  340.3 1.0 copy-start.5
  341.3 0.9 copy-start.6
where the time goes:
time: 351 us; the launch traced here: 350 us
  Pallas kernels  331 us (94%)
  local copies, waits for them, and re-layouts  16.7 us (5%)
    pallas_call x1, Pallas kernels, shards_kernel(): pl.pallas_call(functools.partial(block_kernel, dims), out_shape=shapes, i...  325 us
    unnamed x14, local copies, waits for them, and re-layouts  8.52 us

commit v1 on v0

--- a/solution.py
+++ b/solution.py
@@ -162,7 +162,6 @@
     ain,
     cotb,
     plb,
-    plt,
     smb,
     vec,
     bqkv,
@@ -196,6 +195,10 @@
     dkv,
     smg,
     sg8,
+    hq,
+    hp,
+    h1,
+    h2,
     sems,
     local_sems,
 ):
@@ -211,8 +214,17 @@
     k = f % 2
     j = f // 2
     partner = f + 1 - 2 * k
-    seq_to = [(me + o) % n for o in range(n)]
-    seq_from = [(me + n - o) % n for o in range(n)]
+    x = me % 2
+    y = me // 2
+
+    def peer(o):
+        return (y + o // 2) % 2 * 2 + (x + o % 2) % 2
+
+    seq_to = [peer(o) for o in range(n)]
+    seq_from = seq_to
+    near_x, near_y, across = seq_to[1], seq_to[2], seq_to[3]
+    edge = (j == 0) | (j == J - 1)
+    middle = (j > 0) & (j < J - 1)
     z_to = [2 * ((j + d) % J) + k for d in range(J)]
     z_from = [2 * ((j + J - d) % J) + k for d in range(J)]
     used = {"remote": 0, "local": 0}
@@ -222,8 +234,8 @@
         used["remote"] += count
         return used["remote"] - count
 
-    def send(src, dst, where, recv, late=True):
-        copy = pltpu.make_async_remote_copy(
+    def remote(src, dst, where, recv):
+        return pltpu.make_async_remote_copy(
             src_ref=src,
             dst_ref=dst,
             send_sem=sems.at[take()],
@@ -231,6 +243,12 @@
             device_id=where,
             device_id_type=MESH,
         )
+
+    def when(condition, action):
+        pl.when(condition)(action)
+
+    def send(src, dst, where, recv, late=True):
+        copy = remote(src, dst, where, recv)
         copy.start()
         if late:
             leftover.append(copy)
@@ -267,12 +285,37 @@
         pl.semaphore_signal(barrier, inc=1, device_id={"fsdp": (f + o) % F}, device_id_type=MESH)
     pl.semaphore_wait(barrier, n - 1 + F - 1)
 
-    tok_copies = []
-    for o in range(1, n):
-        where = {"seq": seq_to[o]}
-        c1 = send(plc_in, plb.at[me], where, take())
-        c2 = send(tok_in, tokb.at[me], where, take())
-        tok_copies.append((c1, c2))
+    class Spread:
+        def __init__(self, src, at, rows):
+            self.at, self.rows = at, rows
+            self.first = [
+                send(src, at(me, 0, rows), {"seq": seq_to[o]}, take()) for o in (1, 2)
+            ]
+
+        def relay(self):
+            half = self.rows // 2
+            self.first[0].wait_recv()
+            part = self.at(near_x, 0, half)
+            one = send(part, part, {"seq": near_y}, take(), late=False)
+            self.first[1].wait_recv()
+            part = self.at(near_y, half, self.rows)
+            self.second = [one, send(part, part, {"seq": near_x}, take(), late=False)]
+
+        def finish(self):
+            for copy in self.second:
+                copy.wait_recv()
+
+        def drain(self):
+            for copy in self.second:
+                copy.wait_send()
+
+    def rows_in(ref):
+        return lambda index, lo, hi: ref.at[index, lo:hi]
+
+    plc_copies = [
+        send(plc_in, plb.at[me], {"seq": seq_to[o]}, take()) for o in range(1, n)
+    ]
+    tok = Spread(tok_in, rows_in(tokb), T)
     own_tok = load(tok_in, tokb.at[me])
     own_plc = load(plc_in, plb.at[me])
     own_small = load(small_in, smb.at[f])
@@ -281,20 +324,31 @@
         def __init__(self, src, buf, rows):
             self.buf, self.rows = buf, rows
             self.own = None
+            mine = band(buf, f, rows)
             if src is None:
-                src = band(buf, f, rows)
+                src = mine
             else:
-                self.own = load(src, band(buf, f, rows))
-            self.near = send(src, band(buf, f, rows), {"fsdp": partner}, take(), late=False)
-            self.far = [
-                send(src, band(buf, f, rows), {"fsdp": z_to[d]}, take(), late=False)
-                for d in range(1, J)
-            ]
+                self.own = load(src, mine)
+            self.near = send(src, mine, {"fsdp": partner}, take(), late=False)
+            landed = {d: take() for d in (1, 2, 3)}
+            self.far = {d: remote(src, mine, {"fsdp": z_to[d]}, landed[d]) for d in (1, 2, 3)}
+            when(j != J - 1, self.far[1].start)
+            when(j != 0, self.far[3].start)
+            self.far[2].start()
+            part = band(buf, z_from[2], rows)
+            self.down = remote(part, part, {"fsdp": k}, landed[1])
+            self.up = remote(part, part, {"fsdp": 2 * (J - 1) + k}, landed[3])
             self.relayed = []
 
+        def hop(self):
+            self.far[2].wait_recv()
+            when(j == 1, self.down.start)
+            when(j == J - 2, self.up.start)
+
         def relay(self):
-            for d in range(1, J):
-                self.far[d - 1].wait_recv()
+            for d in (2, 1, 3):
+                if d != 2:
+                    self.far[d].wait_recv()
                 part = band(self.buf, z_from[d], self.rows)
                 self.relayed.append(send(part, part, {"fsdp": partner}, take(), late=False))
 
@@ -306,8 +360,12 @@
                 copy.wait_recv()
 
         def drain(self):
-            for copy in [self.near] + self.far + self.relayed:
+            for copy in [self.near, self.far[2]] + self.relayed:
                 copy.wait_send()
+            when(j != J - 1, self.far[1].wait_send)
+            when(j != 0, self.far[3].wait_send)
+            when(j == 1, self.down.wait_send)
+            when(j == J - 2, self.up.wait_send)
 
     def cut_columns(target, lines):
         for m in range(n):
@@ -325,7 +383,6 @@
         copy.wait()
     cut_columns(wqc, lambda m: [d24[t, :, m * hw : (m + 1) * hw] for t in range(3)])
     weight_q = Weight(None, wqc, R)
-    weight_p = Weight(wp_in, wp, R)
     for copy in raw_1:
         copy.wait()
     cut_columns(
@@ -335,9 +392,6 @@
             for b in range(F)
         ],
     )
-    weight_1 = Weight(None, w1, R)
-    weight_2 = Weight(w2_in.at[rows_of(me, R)], w2, R)
-    own_cot = load(cot_in, cotb.at[me])
 
     own_small.wait()
     for copy in small_copies:
@@ -364,14 +418,35 @@
     def vector(row):
         return vec[row : row + 1, :]
 
+    def rows_of_block(i, rows):
+        return pl.ds(pl.multiple_of(i * T + rows.start, strip), strip)
+
+    def norm_one(i):
+        def body(rows):
+            normed, _ = moments(tokb[i, rows, :].astype(F32))
+            ain[rows_of_block(i, rows), :] = (normed * vector(0) + vector(1)).astype(BF)
+
+        strips(T, strip, body)
+
+    own_tok.wait()
+    norm_one(me)
+    tok.relay()
+    weight_q.hop()
+    weight_p = Weight(wp_in, wp, R)
+    weight_1 = Weight(None, w1, R)
+    own_cot = load(cot_in, cotb.at[me])
+    cot = Spread(cot_in, rows_in(cotb), T)
+    norm_one(near_x)
+    norm_one(near_y)
+
     own_plc.wait()
-    for c1, _ in tok_copies:
-        c1.wait_recv()
+    for copy in plc_copies:
+        copy.wait_recv()
 
     def table(i, carry):
         rows = rows_of(i, T)
         turned = jnp.transpose(plb[i], (1, 0))
-        plt[rows, :] = turned
+        lse[rows, hl : hl + 8] = turned
         angle = turned[:, 1:2] * wave_in[0:1, :] + turned[:, 2:3] * wave_in[1:2, :]
         cosb[rows, :] = jnp.cos(angle)
         sinb[rows, :] = jnp.sin(angle) * wave_in[2:3, :]
@@ -386,21 +461,8 @@
             low_half, pltpu.roll(value, W - HD // 2, 1), pltpu.roll(value, HD // 2, 1)
         )
 
-    def norm_one(i):
-        def body(rows):
-            normed, _ = moments(tokb[i, rows, :].astype(F32))
-            ain[rows_of_block(i, rows), :] = (normed * vector(0) + vector(1)).astype(BF)
-
-        strips(T, strip, body)
-
-    def rows_of_block(i, rows):
-        return pl.ds(pl.multiple_of(i * T + rows.start, strip), strip)
-
-    own_tok.wait()
-    norm_one(me)
-    for o in range(1, n):
-        tok_copies[o - 1][1].wait_recv()
-        norm_one(seq_from[o])
+    tok.finish()
+    norm_one(across)
 
     weight_q.relay()
     weight_q.finish()
@@ -430,7 +492,7 @@
 
     def masked(scores, i):
         ids = jnp.concatenate([plb[b, 3:4, :] for b in range(n)], axis=1)
-        own_ids = plt[rows_of(i, T), 3:4]
+        own_ids = lse[rows_of(i, T), hl + 3 : hl + 4]
         return jnp.where(own_ids == ids, scores * scale, MASKED)
 
     mix_send, mix_recv = take(n * (n - 1)), take(n * (n - 1))
@@ -448,7 +510,7 @@
     def attend_block(i, carry):
         rows = rows_of(i, T)
         outs = []
-        logs = jnp.zeros((T, W), F32)
+        logs = lse[rows, :]
         for h in range(hl):
             q = qkv[rows, h * W : (h + 1) * W]
             kk = qkv[:, QW + h * W : QW + (h + 1) * W]
@@ -465,26 +527,31 @@
             mix_copy(i, o, seq_to[o], me).start()
         return carry
 
-    lax.fori_loop(0, n, attend_block, 0)
-    cot_copies = [
-        send(cot_in, cotb.at[me], {"seq": seq_to[o]}, take()) for o in range(1, n)
-    ]
-
+    weight_p.hop()
+    weight_2 = Weight(w2_in.at[rows_of(me, R)], w2, R)
+    cot.relay()
+    lax.fori_loop(0, n // 2, attend_block, 0)
     weight_p.relay()
+    lax.fori_loop(n // 2, n, attend_block, 0)
+    weight_1.hop()
     weight_p.finish()
-
-    def branch(t, carry):
-        i = (me + 1 + t) % n
+    tok.drain()
+
+    def branch(i, carry):
         rows = rows_of(i, T)
         for o in range(1, n):
             mix_copy(i, o, seq_to[o], seq_from[o]).wait_recv()
         mix[rows, :] = jnp.concatenate([mixc[c, i][:, :hw] for c in range(n)], axis=1)
-        mid[...] = mm(mix[rows, :], wp[...])
+        gmd[...] = mm(mix[rows, :], wp[...])
 
         def body(part):
             whole = rows_of_block(i, part)
-            value = mid[part, :] + tokb[i, part, :].astype(F32) + vector(2)
-            mid[part, :] = value
+            value = gmd[part, :] + tokb[i, part, :].astype(F32) + vector(2)
+
+            @pl.when(i == me)
+            def _():
+                mid[part, :] = value
+
             normed, _ = moments(value)
             mlp[whole, :] = (normed * vector(3) + vector(4)).astype(BF)
 
@@ -493,6 +560,7 @@
 
     lax.fori_loop(0, n, branch, 0)
 
+    weight_2.hop()
     weight_1.relay()
     weight_1.finish()
 
@@ -507,8 +575,8 @@
     lax.fori_loop(0, n, up, 0)
 
     own_cot.wait()
-    for copy in cot_copies:
-        copy.wait_recv()
+    cot.finish()
+    cot.drain()
     weight_2.relay()
     weight_2.finish()
 
@@ -546,7 +614,7 @@
     scatter_mlp = Scatter(snd)
 
     def back(t, carry):
-        i = (me + 1 + t) % n
+        i = peer(t + 1)
         rows = rows_of(i, T)
         grad = (mm_nt(cotb[i], w2[...]) * dge[rows, :].astype(F32)).astype(BF)
         dge[rows, :] = grad
@@ -557,67 +625,105 @@
     lax.fori_loop(0, n, back, 0)
 
     class Gradient:
-        def __init__(self, grad, other, far, result, lanes):
-            self.grad, self.other, self.far, self.result = grad, other, far, result
-            self.lanes = lanes
+        def __init__(self, grad, other, far, extra, result, lo, width):
+            self.grad, self.other, self.far, self.extra = grad, other, far, extra
+            self.result, self.lanes = result, slice(lo, lo + width)
+
+        def of(self, index):
+            return self.grad.at[rows_of(index, R), self.lanes]
 
         def exchange(self):
-            self.near = []
-            for c in range(J):
-                self.near.append(
-                    send(
-                        band(self.grad, 2 * c + 1 - k, R),
-                        self.other.at[c],
-                        {"fsdp": partner},
-                        take(),
-                    )
+            self.near = [
+                send(
+                    self.of(2 * c + 1 - k),
+                    self.other.at[c, :, self.lanes],
+                    {"fsdp": partner},
+                    take(),
                 )
+                for c in range(J)
+            ]
 
         def add_near(self):
             for copy in self.near:
                 copy.wait_recv()
+            lanes = self.lanes
 
             def chip(c, carry):
                 rows = rows_of(2 * c + k, R)
-                self.grad[rows, :] = (
-                    self.grad[rows, :].astype(F32) + self.other[c].astype(F32)
+                self.grad[rows, lanes] = (
+                    self.grad[rows, lanes].astype(F32) + self.other[c, :, lanes].astype(F32)
                 ).astype(BF)
                 return carry
 
             lax.fori_loop(0, J, chip, 0)
-            self.across = [
-                send(
-                    band(self.grad, z_to[d], R),
-                    self.far.at[d - 1],
-                    {"fsdp": z_to[d]},
-                    take(),
+            self.pass_on = remote(
+                self.of(2 * (J - 1 - j) + k),
+                self.extra.at[:, lanes],
+                {"fsdp": 2 * (1 + j // (J - 1)) + k},
+                take(),
+            )
+            self.across = {
+                d: remote(
+                    self.of(z_to[d]), self.far.at[d - 1, :, lanes], {"fsdp": z_to[d]}, take()
                 )
-                for d in range(1, J)
-            ]
+                for d in (1, 2, 3)
+            }
+            when(edge, self.pass_on.start)
+            when(edge, self.across[2].start)
+            when(j != J - 1, self.across[1].start)
+            when(j != 0, self.across[3].start)
+
+        def hop(self):
+            @pl.when(middle)
+            def _():
+                self.pass_on.wait_recv()
+                rows = rows_of(z_to[2], R)
+                self.grad[rows, self.lanes] = (
+                    self.grad[rows, self.lanes].astype(F32)
+                    + self.extra[:, self.lanes].astype(F32)
+                ).astype(BF)
+                self.across[2].start()
 
         def add_far(self):
-            for copy in self.across:
-                copy.wait_recv()
-            rows = rows_of(f, R)
-            total = self.grad[rows, :].astype(F32)
-            for d in range(J - 1):
-                total = total + self.far[d].astype(F32)
-            self.other[0] = total.astype(BF)
-            mine = self.other.at[0]
-            self.keep = load(mine, self.result.at[me])
-            self.share = [
-                send(mine, self.result.at[me], {"seq": seq_to[o]}, take()) for o in range(1, n)
-            ]
+            def total_of(steps):
+                def action():
+                    for d in steps:
+                        self.across[d].wait_recv()
+                    total = self.grad[rows_of(f, R), self.lanes].astype(F32)
+                    for d in steps:
+                        total = total + self.far[d - 1, :, self.lanes].astype(F32)
+                    self.other[0, :, self.lanes] = total.astype(BF)
+
+                return action
+
+            when(j == 0, total_of((2, 3)))
+            when(middle, total_of((1, 2, 3)))
+            when(j == J - 1, total_of((1, 2)))
+
+        def share(self):
+            mine = self.other.at[0, :, self.lanes]
+            self.keep = load(mine, self.result.at[me, :, self.lanes])
+            self.spread = Spread(
+                mine, lambda index, lo, hi: self.result.at[index, lo:hi, self.lanes], R
+            )
+
+        def relay(self):
+            self.spread.relay()
 
         def finish(self):
             self.keep.wait()
-            for copy in self.share:
-                copy.wait_recv()
-
-    grad_up = Gradient(w1, d14, z13, r1_ref, P1)
-    grad_down = Gradient(w2, d24, z23, r2_ref, D)
-    grad_proj = Gradient(gp, dp4, zp3, rp_ref, HP)
-    grad_qkv = Gradient(wqc, dq4, zq3, rq_ref, CQ)
+            self.spread.finish()
+            self.spread.drain()
+            self.across[2].wait_send()
+            when(j != J - 1, self.across[1].wait_send)
+            when(j != 0, self.across[3].wait_send)
+            when(edge, self.pass_on.wait_send)
+
+    CH = CQ // 2
+    grad_up = Gradient(w1, d14, z13, h1, r1_ref, 0, P1)
+    grad_down = Gradient(w2, d24, z23, h2, r2_ref, 0, D)
+    grad_proj = Gradient(gp, dp4, zp3, hp, rp_ref, 0, HP)
+    grad_qkv = [Gradient(wqc, dq4, zq3, hq, rq_ref, b * CH, CH) for b in range(2)]
 
     weight_1.drain()
     weight_2.drain()
@@ -647,6 +753,7 @@
 
     lax.fori_loop(0, P1 // tile, down_grad, 0)
     grad_down.exchange()
+    grad_up.add_near()
 
     smg[...] = jnp.zeros(smg.shape, F32)
     scatter_mlp.wait_recv()
@@ -695,14 +802,56 @@
     mixc[1, me] = mixc[0, me]
     mixc[3, me] = mixc[2, me]
 
-    grad_up.add_near()
     grad_down.add_near()
+    grad_up.hop()
 
     for copy in head_copies:
         copy.wait_recv()
     out_copies = [
         send(band(mlp, seq_to[o], T), tokb.at[me], {"seq": seq_to[o]}, take()) for o in range(1, n)
     ]
+
+    def proj_grad(t, carry):
+        lanes = rows_of(t, tile)
+        total = mm_tn(mix[0:T, lanes], mixc[3, 0])
+        for b in range(1, n):
+            total = total + mm_tn(mix[b * T : (b + 1) * T, lanes], mixc[3, b])
+        gp[lanes, :] = total.astype(BF)
+        return carry
+
+    def qkv_grad(half):
+        pair = hl // 2 * W
+
+        def body(t, carry):
+            rows = rows_of(t, tile)
+            parts = []
+            for third in range(3):
+                at = third * QW + half * pair
+                total = mm_tn(ain[:, rows], qkv[:, at : at + pair])
+                parts += [total[:, h * W : h * W + HD].astype(BF) for h in range(hl // 2)]
+            wqc[rows, half * CH : (half + 1) * CH] = lane_pad(jnp.concatenate(parts, axis=1), CH)
+            return carry
+
+        lax.fori_loop(0, D // tile, body, 0)
+        grad_qkv[half].exchange()
+
+    def between(h):
+        if h == 0:
+            grad_down.hop()
+            for copy in branch_copies:
+                copy.wait_recv()
+            lax.fori_loop(0, D // tile, proj_grad, 0)
+            grad_proj.exchange()
+        if h == 1:
+            grad_proj.add_near()
+            qkv_grad(0)
+            grad_up.add_far()
+        if h == 2:
+            grad_proj.hop()
+            grad_qkv[0].add_near()
+        if h == 3:
+            grad_qkv[0].hop()
+            grad_down.add_far()
 
     for h in range(hl):
         q_at = slice(h * W, (h + 1) * W)
@@ -735,12 +884,13 @@
             return carry
 
         lax.fori_loop(0, n, turn_back, 0)
+        between(h)
 
     scatter_mlp.wait_send()
     scatter_attn = Scatter(snd)
 
     def attn_back(t, carry):
-        i = (me + 1 + t) % n
+        i = peer(t + 1)
         rows = rows_of(i, T)
         snd[rows, :] = mm_nt(qkv[rows, :], wq[...]).astype(BF)
         scatter_attn.start(t, i)
@@ -748,35 +898,11 @@
 
     lax.fori_loop(0, n, attn_back, 0)
 
-    def qkv_grad(t, carry):
-        rows = rows_of(t, tile)
-        total = mm_tn(ain[:, rows], qkv[...])
-        wqc[rows, :] = lane_pad(
-            jnp.concatenate([total[:, h * W : h * W + HD].astype(BF) for h in range(3 * hl)], axis=1),
-            CQ,
-        )
-        return carry
-
-    lax.fori_loop(0, D // tile, qkv_grad, 0)
-    grad_qkv.exchange()
-
-    for copy in branch_copies:
-        copy.wait_recv()
-
-    def proj_grad(t, carry):
-        lanes = rows_of(t, tile)
-        total = mm_tn(mix[0:T, lanes], mixc[3, 0])
-        for b in range(1, n):
-            total = total + mm_tn(mix[b * T : (b + 1) * T, lanes], mixc[3, b])
-        gp[lanes, :] = total.astype(BF)
-        return carry
-
-    lax.fori_loop(0, D // tile, proj_grad, 0)
-    grad_proj.exchange()
-    grad_qkv.add_near()
-    grad_proj.add_near()
-    grad_up.add_far()
-    grad_down.add_far()
+    grad_up.share()
+    grad_down.share()
+    qkv_grad(1)
+    grad_proj.add_far()
+    grad_proj.share()
 
     def bias_sums(part):
         smg[6:7, :] = smg[6:7, :] + jnp.sum(dge[part, :].astype(F32), axis=0, keepdims=True)
@@ -786,7 +912,11 @@
         )
         smg[7:8, :] = smg[7:8, :] + line
 
+    grad_qkv[1].add_near()
     strips(L, 64, bias_sums)
+    grad_qkv[0].add_far()
+    grad_qkv[0].share()
+    grad_qkv[1].hop()
 
     scatter_attn.wait_recv()
 
@@ -808,6 +938,10 @@
         send(smg, sg8.at[f], {"fsdp": (f + o) % F}, take()) for o in range(1, F)
     ]
     sg8[f] = smg[...]
+    grad_up.relay()
+    grad_down.relay()
+    grad_qkv[1].add_far()
+    grad_qkv[1].share()
 
     for copy in out_copies:
         copy.wait_recv()
@@ -835,9 +969,10 @@
         send(vec, sums_ref.at[me], {"seq": seq_to[o]}, take()) for o in range(1, n)
     ]
 
-    grad_qkv.add_far()
-    grad_proj.add_far()
-    for item in (grad_up, grad_down, grad_proj, grad_qkv):
+    grads = [grad_up, grad_down, grad_proj] + grad_qkv
+    for item in grads[2:]:
+        item.relay()
+    for item in grads:
         item.finish()
     for copy in sums_share:
         copy.wait_recv()
@@ -916,7 +1051,12 @@
     loads[2].wait()
     for t in range(3):
         stage[2 * n + t] = jnp.concatenate(
-            [rq[m, :, t * hw : (t + 1) * hw] for m in range(n)], axis=1
+            [
+                rq[m, :, b * CQ // 2 + t * hw // 2 : b * CQ // 2 + (t + 1) * hw // 2]
+                for m in range(n)
+                for b in range(2)
+            ],
+            axis=1,
         ).astype(F32)
         store(stage.at[2 * n + t], qkv_ref.at[:, t * D : (t + 1) * D])
     loads[3].wait()
@@ -993,19 +1133,18 @@
     def pick(value, axis):
         return lax.dynamic_index_in_dim(value, me, axis, keepdims=False)
 
-    small = jnp.concatenate(
-        [
-            norm1_gain,
-            norm1_bias,
-            proj_bias,
-            norm2_gain,
-            norm2_bias,
-            fc2_bias,
-            pick(fc1_bias.reshape(n, part), 0),
-            qkv_bias,
-        ]
+    lines = (
+        norm1_gain,
+        norm1_bias,
+        proj_bias,
+        norm2_gain,
+        norm2_bias,
+        fc2_bias,
+        pick(fc1_bias.reshape(n, part), 0),
+        qkv_bias,
     )
-    small = jnp.pad(small.astype(F32).reshape(10, R), ((0, 6), (0, 0)))
+    small = jnp.concatenate([item.astype(F32).reshape(-1, R) for item in lines])
+    small = jnp.pad(small, ((0, 6), (0, 0)))
     spot = jnp.arange(T, dtype=jnp.int32) + me * T
     ids = jnp.where(picture_ids[0] >= 0, picture_ids[0], -1 - spot)
     places = jnp.stack([picture_ids[0], patch_rows[0], patch_cols[0], ids]).astype(F32)
@@ -1029,7 +1168,6 @@
         vmem((L, D)),
         vmem((n, T, D)),
         vmem((n, 8, T), F32),
-        vmem((L, 8), F32),
         vmem((F, 16, R), F32),
         vmem((8, D), F32),
         vmem((8, 3 * hl * W), F32),
@@ -1063,7 +1201,11 @@
         vmem((L, 2 * W), F32),
         vmem((8, D), F32),
         vmem((F, 8, D), F32),
-        pltpu.SemaphoreType.DMA((320,)),
+        vmem((R, CQ)),
+        vmem((R, HP)),
+        vmem((R, P1)),
+        vmem((R, D)),
+        pltpu.SemaphoreType.DMA((448,)),
         pltpu.SemaphoreType.DMA((24,)),
     ]
     shapes = (
@@ -1112,7 +1254,7 @@
             pltpu.SemaphoreType.DMA((7,)),
             pltpu.SemaphoreType.DMA((7 + 2 * n,)),
         ],
-        compiler_params=pltpu.CompilerParams(vmem_limit_bytes=40000000),
+        compiler_params=pltpu.CompilerParams(vmem_limit_bytes=67043328),
     )(block_out, tokens_grad, rq, rp, r1, r2, sums)
     return (
         block_out[None],

time: 351 us -> 307 us (0.87)
  Pallas kernels: 331 us -> 293 us
  local copies, waits for them, and re-layouts: 16.7 us -> 10.5 us
    pallas_call x1, Pallas kernels: 325 us -> 287 us  [shards_kernel(): pl.pallas_call(functools.partial(block_kernel, dims), out_shape=shapes, i...]
    unnamed x14 -> x0, local copies, waits for them, and re-layouts: 8.52 us -> none
    reshape x0 -> x7, local copies, waits for them, and re-layouts: none -> 4.71 us  [shards_kernel(): small = jnp.concatenate([item.astype(F32).reshape(-1, R) for item in lines])]
    concatenate x1, local copies, waits for them, and re-layouts: 4.79 us -> 0.12 us  [shards_kernel(): small = jnp.concatenate([item.astype(F32).reshape(-1, R) for item in lines])]
where the time goes in v1:
time: 307 us; the launch traced here: 306 us
  Pallas kernels  293 us (95%)
  local copies, waits for them, and re-layouts  10.5 us (3%)
    pallas_call x1, Pallas kernels, shards_kernel(): pl.pallas_call(functools.partial(block_kernel, dims), out_shape=shapes, i...  287 us
    pallas_call x1, Pallas kernels, shards_kernel(): pl.pallas_call(functools.partial(unpack_kernel, dims), out_shape=stored,...  6.17 us

profile of v1, /device:TPU:16, one launch (start us, length us, event | category | flops | bytes accessed | tf_op | source)
XLA Modules:
  0.0 306.1 jit_solution(8416188580258074277)
XLA Ops:
  0.7 0.7 compare_select_fusion
  1.3 0.7 reshape.76
  2.0 0.7 reshape.77
  2.7 0.7 reshape.78
  3.3 0.7 reshape.79
  4.0 0.7 reshape.80
  4.6 0.7 reshape.81
  5.3 0.8 reshape.83
  6.1 0.8 reshape.82
  6.8 0.1 concatenate.4
  7.0 0.7 add_convert_fusion
  7.7 0.6 pad.10.plc_in
  8.3 0.6 pad_convert_fusion.small_in
  8.9 286.7 %shard_map.281 = (bf16[256,1280]{1,0:T(8,128)(2,1)}, f32[256,1280]{1,0:T(8,128)}, bf16[4,160,1024]{2,1,0:T(8,128)(2,1)}, bf16[4,160,384]{2,1,0:T(8,128)(2,1)}, b...) custom-call(bf16[256,1280]{1,0:T(8,128)(2,1)} %bitcast.10, ...), custom_call_target="tpu_custom_call" | custom-call | tf_op jit(solution)/shard_map/pallas_call | solution.py:1220
  295.6 6.2 %shard_map.282 = (bf16[256,1280]{1,0:T(8,128)(2,1)}, f32[256,1280]{1,0:T(8,128)}, f32[160,3840]{1,0:T(8,128)}, f32[160,1280]{1,0:T(8,128)}, f32[160,5120]{1,0:T(...) custom-call(bf16[256,1280]{1,0:T(8,128)(2,1)} %get-tuple-element.28.block_in, f32[256,1280]{1,0:T(8,128)} %get-tuple-element.29.tokens_in, ...), custom_call_target="tpu_custom_call" | custom-call | tf_op jit(solution)/shard_map/pallas_call | solution.py:1239
  301.8 0.7 slice.26
  302.5 0.7 reshape.84
  303.2 0.7 slice.30
  303.9 1.5 fusion
  305.4 0.7 reshape.85
  (1 shorter events, 0.0 us)

commit v2 on v1

--- a/solution.py
+++ b/solution.py
@@ -332,9 +332,9 @@
             self.near = send(src, mine, {"fsdp": partner}, take(), late=False)
             landed = {d: take() for d in (1, 2, 3)}
             self.far = {d: remote(src, mine, {"fsdp": z_to[d]}, landed[d]) for d in (1, 2, 3)}
+            self.far[2].start()
             when(j != J - 1, self.far[1].start)
             when(j != 0, self.far[3].start)
-            self.far[2].start()
             part = band(buf, z_from[2], rows)
             self.down = remote(part, part, {"fsdp": k}, landed[1])
             self.up = remote(part, part, {"fsdp": 2 * (J - 1) + k}, landed[3])
@@ -580,46 +580,87 @@
     weight_2.relay()
     weight_2.finish()
 
+    half = T // 2
+
     class Scatter:
-        def __init__(self, stage):
-            self.stage = stage
-            self.out, self.into = take(n - 1), take(n - 1)
-
-        def copy(self, t, to):
-            return pltpu.make_async_remote_copy(
-                src_ref=band(self.stage, to, T),
-                dst_ref=rsr.at[t],
-                send_sem=sems.at[self.out + t],
-                recv_sem=sems.at[self.into + t],
-                device_id={"seq": to},
-                device_id_type=MESH,
+        def __init__(self, stage, landing, slots):
+            self.stage, self.landing = stage, landing
+            slot_x, slot_y, pass_x, pass_y = slots
+            to_x, to_y = {"seq": near_x}, {"seq": near_y}
+            self.pass_a = self.make(across, 0, pass_x, to_x)
+            self.pass_b = self.make(across, 1, pass_y, to_y)
+            self.last_a = self.make(near_x, 0, slot_x, to_x)
+            self.last_b = self.make(near_y, 1, slot_y, to_y)
+            self.sum_a = self.make(near_y, 0, slot_y, to_y)
+            self.sum_b = self.make(near_x, 1, slot_x, to_x)
+
+        def make(self, block, part, slot, where):
+            return remote(
+                self.stage.at[self.rows(block, part)],
+                self.landing.at[slot, part * half : (part + 1) * half],
+                where,
+                take(),
             )
 
-        def start(self, t, i):
-            @pl.when(t < n - 1)
+        def rows(self, block, part):
+            return pl.ds(pl.multiple_of(block * T + part * half, half), half)
+
+        def start(self, t):
+            @pl.when(t == 0)
             def _():
-                self.copy(t, i).start()
+                self.pass_a.start()
+                self.pass_b.start()
+
+            when(t == 1, self.last_a.start)
+            when(t == 2, self.last_b.start)
+
+        def relay(self, slot):
+            for part, into, out, block in (
+                (0, self.pass_a, self.sum_a, near_y),
+                (1, self.pass_b, self.sum_b, near_x),
+            ):
+                into.wait_recv()
+
+                def body(rows):
+                    at = pl.ds(pl.multiple_of(block * T + part * half + rows.start, strip), strip)
+                    there = pl.ds(pl.multiple_of(part * half + rows.start, strip), strip)
+                    self.stage[at, :] = (
+                        self.stage[at, :].astype(F32) + self.landing[slot, there, :].astype(F32)
+                    ).astype(BF)
+
+                strips(half, strip, body)
+                out.start()
 
         def wait_recv(self):
-            for t in range(n - 1):
-                self.copy(t, seq_to[t + 1]).wait_recv()
+            for copy in (self.last_a, self.last_b, self.sum_a, self.sum_b):
+                copy.wait_recv()
 
         def wait_send(self):
-            for t in range(n - 1):
-                self.copy(t, seq_to[t + 1]).wait_send()
+            for copy in (
+                self.pass_a,
+                self.pass_b,
+                self.last_a,
+                self.last_b,
+                self.sum_a,
+                self.sum_b,
+            ):
+                copy.wait_send()
+
+    def block_at(t):
+        return peer(((t + 2) % 3 + 1) * (1 - t // 3))
 
     for i in range(n):
         for o in range(1, n):
             mix_copy(i, o, seq_to[o], me).wait_send()
-    scatter_mlp = Scatter(snd)
+    scatter_mlp = Scatter(snd, rsr, (0, 1, 2, 2))
 
     def back(t, carry):
-        i = peer(t + 1)
+        i = block_at(t)
         rows = rows_of(i, T)
         grad = (mm_nt(cotb[i], w2[...]) * dge[rows, :].astype(F32)).astype(BF)
         dge[rows, :] = grad
         snd[rows, :] = mm_nt(grad, w1[...]).astype(BF)
-        scatter_mlp.start(t, i)
+        scatter_mlp.start(t)
         return carry
 
     lax.fori_loop(0, n, back, 0)
@@ -735,6 +776,7 @@
 
     lax.fori_loop(0, D // tile, up_grad, 0)
     grad_up.exchange()
+    scatter_mlp.relay(2)
 
     def down(i, carry):
         rows = rows_of(i, T)
@@ -742,6 +784,7 @@
         return carry
 
     lax.fori_loop(0, n, down, 0)
+    grad_up.add_near()
 
     def down_grad(t, carry):
         lanes = rows_of(t, tile)
@@ -753,7 +796,6 @@
 
     lax.fori_loop(0, P1 // tile, down_grad, 0)
     grad_down.exchange()
-    grad_up.add_near()
 
     smg[...] = jnp.zeros(smg.shape, F32)
     scatter_mlp.wait_recv()
@@ -761,9 +803,7 @@
     def gather_parts(part):
         whole = rows_of_block(me, part)
         total = snd[whole, :].astype(F32)
-        for t in range(n - 1):
-            total = total + rsr[t, part, :].astype(F32)
-        return total
+        return total + rsr[0, part, :].astype(F32) + rsr[1, part, :].astype(F32)
 
     def add_sum(row, value):
         smg[row : row + 1, :] = smg[row : row + 1, :] + jnp.sum(value, axis=0, keepdims=True)
@@ -807,9 +847,9 @@
 
     for copy in head_copies:
         copy.wait_recv()
-    out_copies = [
-        send(band(mlp, seq_to[o], T), tokb.at[me], {"seq": seq_to[o]}, take()) for o in range(1, n)
-    ]
+    scatter_out = Scatter(mlp, tokb, (me, me, near_y, near_x))
+    for t in range(n - 1):
+        scatter_out.start(t)
 
     def proj_grad(t, carry):
         lanes = rows_of(t, tile)
@@ -842,6 +882,7 @@
                 copy.wait_recv()
             lax.fori_loop(0, D // tile, proj_grad, 0)
             grad_proj.exchange()
+            scatter_out.relay(across)
         if h == 1:
             grad_proj.add_near()
             qkv_grad(0)
@@ -887,20 +928,21 @@
         between(h)
 
     scatter_mlp.wait_send()
-    scatter_attn = Scatter(snd)
+    scatter_attn = Scatter(snd, rsr, (0, 1, 2, 2))
 
     def attn_back(t, carry):
-        i = peer(t + 1)
+        i = block_at(t)
         rows = rows_of(i, T)
         snd[rows, :] = mm_nt(qkv[rows, :], wq[...]).astype(BF)
-        scatter_attn.start(t, i)
+        scatter_attn.start(t)
         return carry
 
     lax.fori_loop(0, n, attn_back, 0)
 
+    qkv_grad(1)
+    scatter_attn.relay(2)
     grad_up.share()
     grad_down.share()
-    qkv_grad(1)
     grad_proj.add_far()
     grad_proj.share()
 
@@ -943,14 +985,13 @@
     grad_qkv[1].add_far()
     grad_qkv[1].share()
 
-    for copy in out_copies:
-        copy.wait_recv()
+    scatter_out.wait_recv()
 
     def write_out(part):
         whole = rows_of_block(me, part)
         total = mid[part, :] + mlp[whole, :].astype(F32) + vector(5)
-        for o in range(1, n):
-            total = total + tokb[seq_from[o], part, :].astype(F32)
+        for slot in (near_x, near_y):
+            total = total + tokb[slot, part, :].astype(F32)
         bias_rows = rows_of_block(me, part)
         ain[bias_rows, :] = total.astype(BF)
 
@@ -981,8 +1022,10 @@
     block_out.wait()
     weight_p.drain()
     scatter_attn.wait_send()
+    scatter_out.wait_send()
     for copy in leftover:
         copy.wait_send()
+    assert used["remote"] <= sems.shape[0] and used["local"] <= local_sems.shape[0], used
 
 
 def unpack_kernel(

time: 307 us -> 287 us (0.935)
  Pallas kernels: 293 us -> 272 us
    pallas_call x1, Pallas kernels: 287 us -> 266 us  [shards_kernel(): pl.pallas_call(functools.partial(block_kernel, dims), out_shape=shapes, i...]
where the time goes in v2:
time: 287 us; the launch traced here: 285 us
  Pallas kernels  272 us (95%)
  local copies, waits for them, and re-layouts  10.5 us (4%)
    pallas_call x1, Pallas kernels, shards_kernel(): pl.pallas_call(functools.partial(block_kernel, dims), out_shape=shapes, i...  266 us
    pallas_call x1, Pallas kernels, shards_kernel(): pl.pallas_call(functools.partial(unpack_kernel, dims), out_shape=stored,...  6.17 us

profile of v2, /device:TPU:16, one launch (start us, length us, event | category | flops | bytes accessed | tf_op | source)
XLA Modules:
  0.0 285.2 jit_solution(11674314177562741768)
XLA Ops:
  0.7 0.7 compare_select_fusion
  1.3 0.7 reshape.76
  2.0 0.7 reshape.77
  2.7 0.7 reshape.78
  3.3 0.7 reshape.79
  4.0 0.7 reshape.80
  4.6 0.7 reshape.81
  5.3 0.8 reshape.83
  6.1 0.8 reshape.82
  6.8 0.1 concatenate.4
  7.0 0.7 add_convert_fusion
  7.7 0.6 pad.10.plc_in
  8.3 0.6 pad_convert_fusion.small_in
  8.9 265.8 %shard_map.281 = (bf16[256,1280]{1,0:T(8,128)(2,1)}, f32[256,1280]{1,0:T(8,128)}, bf16[4,160,1024]{2,1,0:T(8,128)(2,1)}, bf16[4,160,384]{2,1,0:T(8,128)(2,1)}, b...) custom-call(bf16[256,1280]{1,0:T(8,128)(2,1)} %bitcast.10, ...), custom_call_target="tpu_custom_call" | custom-call | tf_op jit(solution)/shard_map/pallas_call | solution.py:1263
  274.7 6.2 %shard_map.282 = (bf16[256,1280]{1,0:T(8,128)(2,1)}, f32[256,1280]{1,0:T(8,128)}, f32[160,3840]{1,0:T(8,128)}, f32[160,1280]{1,0:T(8,128)}, f32[160,5120]{1,0:T(...) custom-call(bf16[256,1280]{1,0:T(8,128)(2,1)} %get-tuple-element.28.block_in, f32[256,1280]{1,0:T(8,128)} %get-tuple-element.29.tokens_in, ...), custom_call_target="tpu_custom_call" | custom-call | tf_op jit(solution)/shard_map/pallas_call | solution.py:1282
  280.9 0.7 slice.26
  281.6 0.7 reshape.84
  282.3 0.7 slice.30
  283.0 1.5 fusion
  284.5 0.7 reshape.85
  (1 shorter events, 0.0 us)

commit v3 on v2

--- a/solution.py
+++ b/solution.py
@@ -144,8 +144,10 @@
     dims,
     tok_in,
     cot_in,
-    plc_in,
-    small_in,
+    ids_in,
+    row_in,
+    col_in,
+    vec_ins,
     wave_in,
     wq_in,
     wp_in,
@@ -275,6 +277,32 @@
 
     strip = 32
 
+    spot = lax.broadcasted_iota(jnp.int32, (1, T), 1) + me * T
+    ids = ids_in[...]
+    plb[me, 0:4, :] = jnp.concatenate(
+        [
+            ids.astype(F32),
+            row_in[...].astype(F32),
+            col_in[...].astype(F32),
+            jnp.where(ids >= 0, ids, -1 - spot).astype(F32),
+        ],
+        axis=0,
+    )
+    plb[me, 4:8, :] = jnp.zeros((4, T), F32)
+    for row in range(6):
+        smb[f, row : row + 1, :] = vec_ins[row][...].astype(F32).reshape(1, R)
+    up_bias = vec_ins[6][...].astype(F32).reshape(1, n * R)
+    for m in range(n):
+
+        @pl.when(me == m)
+        def _():
+            smb[f, 6:7, :] = up_bias[:, m * R : (m + 1) * R]
+
+    qkv_bias = vec_ins[7][...].astype(F32).reshape(1, 3 * R)
+    for t in range(3):
+        smb[f, 7 + t : 8 + t, :] = qkv_bias[:, t * R : (t + 1) * R]
+    smb[f, 10:16, :] = jnp.zeros((6, R), F32)
+
     raw_q = [load(wq_in.at[:, t * D : (t + 1) * D], d24.at[t]) for t in range(3)]
     raw_1 = [load(w1_in.at[:, c * P1 : (c + 1) * P1], d14.at[c]) for c in range(n)]
 
@@ -313,12 +341,10 @@
         return lambda index, lo, hi: ref.at[index, lo:hi]
 
     plc_copies = [
-        send(plc_in, plb.at[me], {"seq": seq_to[o]}, take()) for o in range(1, n)
+        send(plb.at[me], plb.at[me], {"seq": seq_to[o]}, take()) for o in range(1, n)
     ]
     tok = Spread(tok_in, rows_in(tokb), T)
     own_tok = load(tok_in, tokb.at[me])
-    own_plc = load(plc_in, plb.at[me])
-    own_small = load(small_in, smb.at[f])
 
     class Weight:
         def __init__(self, src, buf, rows):
@@ -367,6 +393,111 @@
             when(j == 1, self.down.wait_send)
             when(j == J - 2, self.up.wait_send)
 
+    class Quarter:
+        def __init__(self):
+            self.cols = pl.ds(pl.multiple_of(x * (D // 2), D // 2), D // 2)
+            self.holder, self.other = y == k, y != k
+            used["local"] += 1
+            self.own = pltpu.make_async_copy(
+                wp_in.at[:, self.cols],
+                wp.at[j, k, :, self.cols],
+                local_sems.at[used["local"] - 1],
+            )
+            when(self.holder, self.own.start)
+            landed = {d: take() for d in (1, 2, 3)}
+            mine = wp.at[j, k, :, self.cols]
+            self.far = {
+                d: remote(wp_in.at[:, self.cols], mine, {"fsdp": z_to[d]}, landed[d])
+                for d in (1, 2, 3)
+            }
+            part = wp.at[z_from[2] // 2, k, :, self.cols]
+            self.down = remote(part, part, {"fsdp": k}, landed[1])
+            self.up = remote(part, part, {"fsdp": 2 * (J - 1) + k}, landed[3])
+            when(self.holder, self.far[2].start)
+            when(self.holder & (j != J - 1), self.far[1].start)
+            when(self.holder & (j != 0), self.far[3].start)
+
+            def quarter(device_y, device_x, lo, hi):
+                cols = pl.ds(pl.multiple_of(device_x * (D // 2), D // 2), D // 2)
+                return wp.at[lo:hi, device_y, :, cols]
+
+            to_x, to_y, to_core = {"seq": near_x}, {"seq": near_y}, {"fsdp": partner}
+            h = J // 2
+            whole = quarter(y, x, 0, J)
+            self.give = [remote(whole, whole, where, take()) for where in (to_x, to_y, to_core)]
+            q = quarter(y, 1 - x, 0, J)
+            self.along_x = remote(q, q, to_core, take())
+            q = quarter(y, 1 - x, 0, h)
+            self.on_y = remote(q, q, to_y, take())
+            q = quarter(1 - y, x, 0, J)
+            self.along_y = remote(q, q, to_core, take())
+            q = quarter(1 - y, x, h, J)
+            self.on_x = remote(q, q, to_x, take())
+            q = quarter(1 - y, 1 - x, 0, J)
+            self.last = remote(q, q, to_core, take())
+
+        def hop(self):
+            @pl.when(self.holder)
+            def _():
+                self.far[2].wait_recv()
+                when(j == 1, self.down.start)
+                when(j == J - 2, self.up.start)
+
+        def start_give(self):
+            @pl.when(self.holder)
+            def _():
+                self.own.wait()
+                self.far[1].wait_recv()
+                self.far[3].wait_recv()
+                for copy in self.give:
+                    copy.start()
+
+        def relay(self):
+            @pl.when(self.holder)
+            def _():
+                self.give[0].wait_recv()
+                self.on_y.start()
+                self.along_x.start()
+
+            @pl.when(self.other)
+            def _():
+                self.give[1].wait_recv()
+                self.on_x.start()
+                self.along_y.start()
+
+        def relay_last(self):
+            @pl.when(self.other)
+            def _():
+                self.on_y.wait_recv()
+                self.on_x.wait_recv()
+                self.last.start()
+
+        def finish(self):
+            @pl.when(self.holder)
+            def _():
+                self.along_y.wait_recv()
+                self.last.wait_recv()
+
+            @pl.when(self.other)
+            def _():
+                self.give[2].wait_recv()
+                self.along_x.wait_recv()
+
+        def drain(self):
+            @pl.when(self.holder)
+            def _():
+                for copy in self.give + [self.along_x, self.on_y, self.far[2]]:
+                    copy.wait_send()
+                when(j != J - 1, self.far[1].wait_send)
+                when(j != 0, self.far[3].wait_send)
+                when(j == 1, self.down.wait_send)
+                when(j == J - 2, self.up.wait_send)
+
+            @pl.when(self.other)
+            def _():
+                for copy in (self.along_y, self.on_x, self.last):
+                    copy.wait_send()
+
     def cut_columns(target, lines):
         for m in range(n):
 
@@ -377,7 +508,7 @@
                 )
 
     small_copies = [
-        send(small_in, smb.at[f], {"fsdp": (f + o) % F}, take()) for o in range(1, F)
+        send(smb.at[f], smb.at[f], {"fsdp": (f + o) % F}, take()) for o in range(1, F)
     ]
     for copy in raw_q:
         copy.wait()
@@ -393,7 +524,6 @@
         ],
     )
 
-    own_small.wait()
     for copy in small_copies:
         copy.wait_recv()
     for row in range(7):
@@ -432,14 +562,13 @@
     norm_one(me)
     tok.relay()
     weight_q.hop()
-    weight_p = Weight(wp_in, wp, R)
+    weight_p = Quarter()
     weight_1 = Weight(None, w1, R)
     own_cot = load(cot_in, cotb.at[me])
     cot = Spread(cot_in, rows_in(cotb), T)
     norm_one(near_x)
     norm_one(near_y)
 
-    own_plc.wait()
     for copy in plc_copies:
         copy.wait_recv()
 
@@ -465,6 +594,7 @@
     norm_one(across)
 
     weight_q.relay()
+    weight_p.hop()
     weight_q.finish()
 
     def spread_heads(rows):
@@ -488,6 +618,7 @@
                 qkv[rows, t * QW + h * W : t * QW + (h + 1) * W] = u.astype(BF)
         return carry
 
+    weight_p.start_give()
     lax.fori_loop(0, n, project, 0)
 
     def masked(scores, i):
@@ -527,22 +658,25 @@
             mix_copy(i, o, seq_to[o], me).start()
         return carry
 
-    weight_p.hop()
     weight_2 = Weight(w2_in.at[rows_of(me, R)], w2, R)
     cot.relay()
     lax.fori_loop(0, n // 2, attend_block, 0)
     weight_p.relay()
+    weight_1.hop()
     lax.fori_loop(n // 2, n, attend_block, 0)
-    weight_1.hop()
+    weight_p.relay_last()
     weight_p.finish()
     tok.drain()
+
+    def proj_weight():
+        return wp[...].reshape(D, D)
 
     def branch(i, carry):
         rows = rows_of(i, T)
         for o in range(1, n):
             mix_copy(i, o, seq_to[o], seq_from[o]).wait_recv()
         mix[rows, :] = jnp.concatenate([mixc[c, i][:, :hw] for c in range(n)], axis=1)
-        gmd[...] = mm(mix[rows, :], wp[...])
+        gmd[...] = mm(mix[rows, :], proj_weight())
 
         def body(part):
             whole = rows_of_block(i, part)
@@ -829,7 +963,7 @@
     strips(T, strip, norm_two_back)
     own_rows = rows_of(me, T)
     low_branch = snd[own_rows, :]
-    grad_mixed = mm_nt(low_branch, wp[...]).astype(BF)
+    grad_mixed = mm_nt(low_branch, proj_weight()).astype(BF)
     for c in range(n):
         mixc[0, c] = lane_pad(grad_mixed[:, c * hw : (c + 1) * hw], HP)
         mixc[2, c] = lane_pad(low_branch[:, c * hw : (c + 1) * hw], HP)
@@ -1043,7 +1177,14 @@
     proj_ref,
     up_ref,
     down_ref,
-    vec_ref,
+    v0,
+    v1,
+    v2,
+    v3,
+    v4,
+    v5,
+    v6,
+    v7,
     block,
     tokens,
     rq,
@@ -1052,7 +1193,6 @@
     r2,
     sums,
     stage,
-    vec,
     in_sems,
     out_sems,
 ):
@@ -1119,16 +1259,18 @@
             total = sums[0, 0:6, own]
             for m in range(1, n):
                 total = total + sums[m, 0:6, own]
-            lines = [total] + [sums[m, 6:7, own] for m in range(n)]
+            for row, out in enumerate((v0, v1, v2, v3, v4, v5)):
+                out[...] = total[row : row + 1, :].reshape(R)
+            lines = [sums[m, 6:7, own] for m in range(n)]
+            v6[...] = jnp.concatenate(lines, axis=1).reshape(n * R)
+            lines = []
             for b in range(3):
                 spot = 3 * s + b
                 third, rest = spot // (n * per_part), spot % (n * per_part)
                 at = third * hw + rest % per_part * R
                 lines.append(sums[rest // per_part, 7:8, at : at + R])
-            lines.append(jnp.zeros((16 - 9 - n, R), F32))
-            vec[...] = jnp.concatenate(lines, axis=0)
-
-    store(vec, vec_ref)
+            v7[...] = jnp.concatenate(lines, axis=1).reshape(3 * R)
+
     for copy in stores:
         copy.wait()
 
@@ -1173,9 +1315,6 @@
     J = F // 2
     W = 128
 
-    def pick(value, axis):
-        return lax.dynamic_index_in_dim(value, me, axis, keepdims=False)
-
     lines = (
         norm1_gain,
         norm1_bias,
@@ -1183,15 +1322,9 @@
         norm2_gain,
         norm2_bias,
         fc2_bias,
-        pick(fc1_bias.reshape(n, part), 0),
+        fc1_bias,
         qkv_bias,
     )
-    small = jnp.concatenate([item.astype(F32).reshape(-1, R) for item in lines])
-    small = jnp.pad(small, ((0, 6), (0, 0)))
-    spot = jnp.arange(T, dtype=jnp.int32) + me * T
-    ids = jnp.where(picture_ids[0] >= 0, picture_ids[0], -1 - spot)
-    places = jnp.stack([picture_ids[0], patch_rows[0], patch_cols[0], ids]).astype(F32)
-    places = jnp.pad(places, ((0, 4), (0, 0)))
     quarter = HD // 4
     inverse = 10000.0 ** (-np.arange(quarter) / quarter)
     wave = np.zeros((8, W), np.float32)
@@ -1218,7 +1351,7 @@
         vmem((L, W), F32),
         vmem((D, CQ)),
         vmem((D, 3 * hl * W)),
-        vmem((D, D)),
+        vmem((J, 2, R, D)),
         vmem((D, P1)),
         vmem((P1, D)),
         vmem((L, 3 * hl * W)),
@@ -1263,13 +1396,25 @@
     block_out, tokens_grad, rq, rp, r1, r2, sums = pl.pallas_call(
         functools.partial(block_kernel, dims),
         out_shape=shapes,
-        in_specs=[anywhere] * 4 + [local] + [anywhere] * 4,
+        in_specs=[anywhere] * 2 + [local] * 3 + [(local,) * 8] + [local] + [anywhere] * 4,
         out_specs=[anywhere] * 7,
         scratch_shapes=scratch,
         compiler_params=pltpu.CompilerParams(
             collective_id=0, has_side_effects=True, vmem_limit_bytes=67043328
         ),
-    )(tokens[0], cotangent[0], places, small, wave, qkv_weight, proj_weight, fc1_weight, fc2_weight)
+    )(
+        tokens[0],
+        cotangent[0],
+        picture_ids,
+        patch_rows,
+        patch_cols,
+        lines,
+        wave,
+        qkv_weight,
+        proj_weight,
+        fc1_weight,
+        fc2_weight,
+    )
     stored = (
         jax.ShapeDtypeStruct((T, D), BF),
         jax.ShapeDtypeStruct((T, D), F32),
@@ -1277,13 +1422,12 @@
         jax.ShapeDtypeStruct((R, D), F32),
         jax.ShapeDtypeStruct((R, hidden), F32),
         jax.ShapeDtypeStruct((n * R, D), F32),
-        jax.ShapeDtypeStruct((16, R), F32),
-    )
-    block_out, tokens_grad, full_qkv, full_proj, full_up, full_down, sums = pl.pallas_call(
+    ) + tuple(jax.ShapeDtypeStruct((size,), F32) for size in [R] * 6 + [n * R, 3 * R])
+    block_out, tokens_grad, full_qkv, full_proj, full_up, full_down, *vectors = pl.pallas_call(
         functools.partial(unpack_kernel, dims),
         out_shape=stored,
         in_specs=[anywhere] * 7,
-        out_specs=[anywhere] * 7,
+        out_specs=[anywhere] * 6 + [local] * 8,
         scratch_shapes=[
             vmem((T, D)),
             vmem((T, D), F32),
@@ -1293,7 +1437,6 @@
             vmem((n, R, D)),
             vmem((n, 8, D), F32),
             vmem((4 + 2 * n, R, D), F32),
-            vmem((16, R), F32),
             pltpu.SemaphoreType.DMA((7,)),
             pltpu.SemaphoreType.DMA((7 + 2 * n,)),
         ],
@@ -1302,18 +1445,18 @@
     return (
         block_out[None],
         tokens_grad[None],
-        sums[0],
-        sums[1],
+        vectors[0],
+        vectors[1],
         full_qkv,
-        sums[6 + n : 9 + n].reshape(3 * R),
+        vectors[7],
         full_proj,
-        sums[2],
-        sums[3],
-        sums[4],
+        vectors[2],
+        vectors[3],
+        vectors[4],
         full_up,
-        sums[6 : 6 + n].reshape(n * R),
+        vectors[6],
         full_down,
-        sums[5],
+        vectors[5],
     )
 
 

time: 287 us -> 282 us (0.983)
  local copies, waits for them, and re-layouts: 10.5 us -> 0 us
  Pallas kernels: 272 us -> 280 us
    pallas_call x1, Pallas kernels: 266 us -> 273 us  [shards_kernel(): pl.pallas_call(functools.partial(block_kernel, dims), out_shape=shapes, i...]
    reshape x10 -> x0, local copies, waits for them, and re-layouts: 6.81 us -> none  [the longest x7 4.71 us: shards_kernel(): small = jnp.concatenate([item.astype(F32).reshape(-1, R) for item in lines])]
    slice x3 -> x0, local copies, waits for them, and re-layouts: 2.92 us -> none  [the longest x1 1.5 us: shards_kernel(): sums[5]]
where the time goes in v3:
time: 282 us; the launch traced here: 280 us
  Pallas kernels  280 us (99%)
    pallas_call x1, Pallas kernels, shards_kernel(): pl.pallas_call(functools.partial(block_kernel, dims), out_shape=shapes, i...  273 us
    pallas_call x1, Pallas kernels, shards_kernel(): pl.pallas_call(functools.partial(unpack_kernel, dims), out_shape=stored,...  6.78 us

profile of v3, /device:TPU:16, one launch (start us, length us, event | category | flops | bytes accessed | tf_op | source)
XLA Modules:
  0.0 280.5 jit_solution(9790084503636150602)
XLA Ops:
  0.7 272.9 %shard_map.281 = (bf16[256,1280]{1,0:T(8,128)(2,1)}, f32[256,1280]{1,0:T(8,128)}, bf16[4,160,1024]{2,1,0:T(8,128)(2,1)}, bf16[4,160,384]{2,1,0:T(8,128)(2,1)}, b...) custom-call(bf16[256,1280]{1,0:T(8,128)(2,1)} %bitcast.4, ...), custom_call_target="tpu_custom_call" | custom-call | tf_op jit(solution)/shard_map/pallas_call | solution.py:1396
  273.5 6.8 %shard_map.282 = (bf16[256,1280]{1,0:T(8,128)(2,1)}, f32[256,1280]{1,0:T(8,128)}, f32[160,3840]{1,0:T(8,128)}, f32[160,1280]{1,0:T(8,128)}, f32[160,5120]{1,0:T(...) custom-call(bf16[256,1280]{1,0:T(8,128)(2,1)} %get-tuple-element.35., ...), custom_call_target="tpu_custom_call" | custom-call | tf_op jit(solution)/shard_map/pallas_call | solution.py:1426

commit v4 on v3

--- a/solution.py
+++ b/solution.py
@@ -659,12 +659,12 @@
         return carry
 
     weight_2 = Weight(w2_in.at[rows_of(me, R)], w2, R)
-    cot.relay()
     lax.fori_loop(0, n // 2, attend_block, 0)
     weight_p.relay()
     weight_1.hop()
     lax.fori_loop(n // 2, n, attend_block, 0)
     weight_p.relay_last()
+    cot.relay()
     weight_p.finish()
     tok.drain()
 
@@ -1011,22 +1011,23 @@
 
     def between(h):
         if h == 0:
-            grad_down.hop()
             for copy in branch_copies:
                 copy.wait_recv()
             lax.fori_loop(0, D // tile, proj_grad, 0)
             grad_proj.exchange()
-            scatter_out.relay(across)
         if h == 1:
+            grad_down.hop()
             grad_proj.add_near()
             qkv_grad(0)
+            scatter_out.relay(across)
+        if h == 2:
             grad_up.add_far()
-        if h == 2:
+            grad_up.share()
+            grad_qkv[0].add_near()
             grad_proj.hop()
-            grad_qkv[0].add_near()
         if h == 3:
-            grad_qkv[0].hop()
             grad_down.add_far()
+            grad_down.share()
 
     for h in range(hl):
         q_at = slice(h * W, (h + 1) * W)
@@ -1073,10 +1074,11 @@
 
     lax.fori_loop(0, n, attn_back, 0)
 
+    grad_qkv[0].hop()
     qkv_grad(1)
+    grad_up.relay()
     scatter_attn.relay(2)
-    grad_up.share()
-    grad_down.share()
+    grad_down.relay()
     grad_proj.add_far()
     grad_proj.share()
 
@@ -1114,8 +1116,8 @@
         send(smg, sg8.at[f], {"fsdp": (f + o) % F}, take()) for o in range(1, F)
     ]
     sg8[f] = smg[...]
-    grad_up.relay()
-    grad_down.relay()
+    grad_proj.relay()
+    grad_qkv[0].relay()
     grad_qkv[1].add_far()
     grad_qkv[1].share()
 
@@ -1145,8 +1147,7 @@
     ]
 
     grads = [grad_up, grad_down, grad_proj] + grad_qkv
-    for item in grads[2:]:
-        item.relay()
+    grad_qkv[1].relay()
     for item in grads:
         item.finish()
     for copy in sums_share:

time: 282 us -> 269 us (0.954)
  Pallas kernels: 280 us -> 268 us
    pallas_call x1, Pallas kernels: 273 us -> 261 us  [shards_kernel(): pl.pallas_call(functools.partial(block_kernel, dims), out_shape=shapes, i...]
where the time goes in v4:
time: 269 us
  Pallas kernels  268 us (100%)
    pallas_call x1, Pallas kernels, shards_kernel(): pl.pallas_call(functools.partial(block_kernel, dims), out_shape=shapes, i...  261 us
    pallas_call x1, Pallas kernels, shards_kernel(): pl.pallas_call(functools.partial(unpack_kernel, dims), out_shape=stored,...  6.78 us

profile of v4, /device:TPU:16, one launch (start us, length us, event | category | flops | bytes accessed | tf_op | source)
XLA Modules:
  0.0 268.6 jit_solution(3150000020656178365)
XLA Ops:
  0.7 261.0 %shard_map.281 = (bf16[256,1280]{1,0:T(8,128)(2,1)}, f32[256,1280]{1,0:T(8,128)}, bf16[4,160,1024]{2,1,0:T(8,128)(2,1)}, bf16[4,160,384]{2,1,0:T(8,128)(2,1)}, b...) custom-call(bf16[256,1280]{1,0:T(8,128)(2,1)} %bitcast.4, ...), custom_call_target="tpu_custom_call" | custom-call | tf_op jit(solution)/shard_map/pallas_call | solution.py:1397
  261.7 6.8 %shard_map.282 = (bf16[256,1280]{1,0:T(8,128)(2,1)}, f32[256,1280]{1,0:T(8,128)}, f32[160,3840]{1,0:T(8,128)}, f32[160,1280]{1,0:T(8,128)}, f32[160,5120]{1,0:T(...) custom-call(bf16[256,1280]{1,0:T(8,128)(2,1)} %get-tuple-element.35., ...), custom_call_target="tpu_custom_call" | custom-call | tf_op jit(solution)/shard_map/pallas_call | solution.py:1427

commit v5 on v4

--- a/solution.py
+++ b/solution.py
@@ -626,17 +626,29 @@
         own_ids = lse[rows_of(i, T), hl + 3 : hl + 4]
         return jnp.where(own_ids == ids, scores * scale, MASKED)
 
-    mix_send, mix_recv = take(n * (n - 1)), take(n * (n - 1))
-
-    def mix_copy(i, o, peer, source):
+    mix_send, mix_recv = take(4 * n), take(4 * n)
+
+    def mix_copy(i, spot, part, where):
         return pltpu.make_async_remote_copy(
-            src_ref=mixc.at[source, i],
-            dst_ref=mixc.at[source, i],
-            send_sem=sems.at[mix_send + i * (n - 1) + o - 1],
-            recv_sem=sems.at[mix_recv + i * (n - 1) + o - 1],
-            device_id={"seq": peer},
+            src_ref=part,
+            dst_ref=part,
+            send_sem=sems.at[mix_send + 4 * i + spot],
+            recv_sem=sems.at[mix_recv + 4 * i + spot],
+            device_id={"seq": where},
             device_id_type=MESH,
         )
+
+    def mix_first(i, o, source):
+        return mix_copy(i, o - 1, mixc.at[source, i], seq_to[o])
+
+    def mix_pass(i, o):
+        part = mixc.at[seq_to[o], i, (o - 1) * T // 2 : o * T // 2]
+        return mix_copy(i, o + 1, part, seq_to[3 - o])
+
+    def mix_relay(i):
+        for o in (1, 2):
+            mix_first(i, o, seq_to[o]).wait_recv()
+            mix_pass(i, o).start()
 
     def attend_block(i, carry):
         rows = rows_of(i, T)
@@ -654,8 +666,9 @@
             logs = jnp.where(lane == h, top + jnp.log(total), logs)
         lse[rows, :] = logs
         mixc[me, i] = lane_pad(jnp.concatenate(outs, axis=1), HP)
-        for o in range(1, n):
-            mix_copy(i, o, seq_to[o], me).start()
+        for o in (1, 2):
+            mix_first(i, o, me).start()
+        when(i > 0, lambda: mix_relay(i - 1))
         return carry
 
     weight_2 = Weight(w2_in.at[rows_of(me, R)], w2, R)
@@ -664,7 +677,6 @@
     weight_1.hop()
     lax.fori_loop(n // 2, n, attend_block, 0)
     weight_p.relay_last()
-    cot.relay()
     weight_p.finish()
     tok.drain()
 
@@ -673,8 +685,8 @@
 
     def branch(i, carry):
         rows = rows_of(i, T)
-        for o in range(1, n):
-            mix_copy(i, o, seq_to[o], seq_from[o]).wait_recv()
+        for o in (1, 2):
+            mix_pass(i, o).wait_recv()
         mix[rows, :] = jnp.concatenate([mixc[c, i][:, :hw] for c in range(n)], axis=1)
         gmd[...] = mm(mix[rows, :], proj_weight())
 
@@ -692,7 +704,10 @@
         strips(T, strip, body)
         return carry
 
-    lax.fori_loop(0, n, branch, 0)
+    lax.fori_loop(0, 1, branch, 0)
+    mix_relay(n - 1)
+    cot.relay()
+    lax.fori_loop(1, n, branch, 0)
 
     weight_2.hop()
     weight_1.relay()
@@ -784,8 +799,9 @@
         return peer(((t + 2) % 3 + 1) * (1 - t // 3))
 
     for i in range(n):
-        for o in range(1, n):
-            mix_copy(i, o, seq_to[o], me).wait_send()
+        for o in (1, 2):
+            mix_first(i, o, me).wait_send()
+            mix_pass(i, o).wait_send()
     scatter_mlp = Scatter(snd, rsr, (0, 1, 2, 2))
 
     def back(t, carry):

time: 269 us -> 262 us (0.974)
  Pallas kernels: 268 us -> 260 us
    pallas_call x1, Pallas kernels: 261 us -> 253 us  [shards_kernel(): pl.pallas_call(functools.partial(block_kernel, dims), out_shape=shapes, i...]
where the time goes in v5:
time: 262 us; the launch traced here: 261 us
  Pallas kernels  260 us (99%)
    pallas_call x1, Pallas kernels, shards_kernel(): pl.pallas_call(functools.partial(block_kernel, dims), out_shape=shapes, i...  253 us
    pallas_call x1, Pallas kernels, shards_kernel(): pl.pallas_call(functools.partial(unpack_kernel, dims), out_shape=stored,...  6.78 us

profile of v5, /device:TPU:16, one launch (start us, length us, event | category | flops | bytes accessed | tf_op | source)
XLA Modules:
  0.0 260.8 jit_solution(16733460734633956485)
XLA Ops:
  0.7 253.2 %shard_map.281 = (bf16[256,1280]{1,0:T(8,128)(2,1)}, f32[256,1280]{1,0:T(8,128)}, bf16[4,160,1024]{2,1,0:T(8,128)(2,1)}, bf16[4,160,384]{2,1,0:T(8,128)(2,1)}, b...) custom-call(bf16[256,1280]{1,0:T(8,128)(2,1)} %bitcast.4, ...), custom_call_target="tpu_custom_call" | custom-call | tf_op jit(solution)/shard_map/pallas_call | solution.py:1413
  253.8 6.8 %shard_map.282 = (bf16[256,1280]{1,0:T(8,128)(2,1)}, f32[256,1280]{1,0:T(8,128)}, f32[160,3840]{1,0:T(8,128)}, f32[160,1280]{1,0:T(8,128)}, f32[160,5120]{1,0:T(...) custom-call(bf16[256,1280]{1,0:T(8,128)(2,1)} %get-tuple-element.35., ...), custom_call_target="tpu_custom_call" | custom-call | tf_op jit(solution)/shard_map/pallas_call | solution.py:1443

commit v6 on v5

--- a/solution.py
+++ b/solution.py
@@ -674,8 +674,8 @@
     weight_2 = Weight(w2_in.at[rows_of(me, R)], w2, R)
     lax.fori_loop(0, n // 2, attend_block, 0)
     weight_p.relay()
+    lax.fori_loop(n // 2, n, attend_block, 0)
     weight_1.hop()
-    lax.fori_loop(n // 2, n, attend_block, 0)
     weight_p.relay_last()
     weight_p.finish()
     tok.drain()
@@ -707,9 +707,9 @@
     lax.fori_loop(0, 1, branch, 0)
     mix_relay(n - 1)
     cot.relay()
+    weight_2.hop()
     lax.fori_loop(1, n, branch, 0)
 
-    weight_2.hop()
     weight_1.relay()
     weight_1.finish()
 

time: 262 us -> 256 us (0.977)
  Pallas kernels: 260 us -> 254 us
    pallas_call x1, Pallas kernels: 253 us -> 247 us  [shards_kernel(): pl.pallas_call(functools.partial(block_kernel, dims), out_shape=shapes, i...]
where the time goes in v6:
time: 256 us; the launch traced here: 255 us
  Pallas kernels  254 us (99%)
    pallas_call x1, Pallas kernels, shards_kernel(): pl.pallas_call(functools.partial(block_kernel, dims), out_shape=shapes, i...  247 us
    pallas_call x1, Pallas kernels, shards_kernel(): pl.pallas_call(functools.partial(unpack_kernel, dims), out_shape=stored,...  6.78 us

profile of v6, /device:TPU:16, one launch (start us, length us, event | category | flops | bytes accessed | tf_op | source)
XLA Modules:
  0.0 255.0 jit_solution(7190020164179552977)
XLA Ops:
  0.7 247.4 %shard_map.281 = (bf16[256,1280]{1,0:T(8,128)(2,1)}, f32[256,1280]{1,0:T(8,128)}, bf16[4,160,1024]{2,1,0:T(8,128)(2,1)}, bf16[4,160,384]{2,1,0:T(8,128)(2,1)}, b...) custom-call(bf16[256,1280]{1,0:T(8,128)(2,1)} %bitcast.4, ...), custom_call_target="tpu_custom_call" | custom-call | tf_op jit(solution)/shard_map/pallas_call | solution.py:1413
  248.0 6.8 %shard_map.282 = (bf16[256,1280]{1,0:T(8,128)(2,1)}, f32[256,1280]{1,0:T(8,128)}, f32[160,3840]{1,0:T(8,128)}, f32[160,1280]{1,0:T(8,128)}, f32[160,5120]{1,0:T(...) custom-call(bf16[256,1280]{1,0:T(8,128)(2,1)} %get-tuple-element.35., ...), custom_call_target="tpu_custom_call" | custom-call | tf_op jit(solution)/shard_map/pallas_call | solution.py:1443

commit v7 on v6

--- a/solution.py
+++ b/solution.py
@@ -707,10 +707,11 @@
     lax.fori_loop(0, 1, branch, 0)
     mix_relay(n - 1)
     cot.relay()
+    lax.fori_loop(1, 2, branch, 0)
     weight_2.hop()
-    lax.fori_loop(1, n, branch, 0)
-
     weight_1.relay()
+    lax.fori_loop(2, n, branch, 0)
+
     weight_1.finish()
 
     def up(i, carry):

time: 256 us -> 256 us (level)
  no operation moved by 1% of the time
where the time goes in v7:
time: 256 us; the launch traced here: 255 us
  Pallas kernels  254 us (99%)
    pallas_call x1, Pallas kernels, shards_kernel(): pl.pallas_call(functools.partial(block_kernel, dims), out_shape=shapes, i...  247 us
    pallas_call x1, Pallas kernels, shards_kernel(): pl.pallas_call(functools.partial(unpack_kernel, dims), out_shape=stored,...  6.78 us

profile of v7, /device:TPU:16, one launch (start us, length us, event | category | flops | bytes accessed | tf_op | source)
XLA Modules:
  0.0 254.6 jit_solution(10028969699920086122)
XLA Ops:
  0.7 246.9 %shard_map.281 = (bf16[256,1280]{1,0:T(8,128)(2,1)}, f32[256,1280]{1,0:T(8,128)}, bf16[4,160,1024]{2,1,0:T(8,128)(2,1)}, bf16[4,160,384]{2,1,0:T(8,128)(2,1)}, b...) custom-call(bf16[256,1280]{1,0:T(8,128)(2,1)} %bitcast.4, ...), custom_call_target="tpu_custom_call" | custom-call | tf_op jit(solution)/shard_map/pallas_call | solution.py:1414
  247.6 6.8 %shard_map.282 = (bf16[256,1280]{1,0:T(8,128)(2,1)}, f32[256,1280]{1,0:T(8,128)}, f32[160,3840]{1,0:T(8,128)}, f32[160,1280]{1,0:T(8,128)}, f32[160,5120]{1,0:T(...) custom-call(bf16[256,1280]{1,0:T(8,128)(2,1)} %get-tuple-element.35., ...), custom_call_target="tpu_custom_call" | custom-call | tf_op jit(solution)/shard_map/pallas_call | solution.py:1444
